TPU v7x, 32 devices: a whole 2x2x4 slice. The times are simulated.
32 devices in a mesh: dp: 16 (over z, y, core), tensor: 2 (over x).
Axes of the slice: x: 2, y: 2, z: 4, core: 2. Of those that a mesh axis runs over, the one named last changes fastest.
Arguments:
- tokens: bfloat16 [28672, 768], P(('dp', 'tensor')), may hold values from -6 to 6
- cotangent: bfloat16 [28672, 768], P(('dp', 'tensor')), may hold values from -6 to 6
- time_embed: float32 [16, 128], P('dp'), may hold values from -4 to 4
- block_parent: int32 [16, 14], P('dp'), may hold values from 0 to 5, as said below
- positions: int32 [28672], P('dp'), may hold values from 0 to 511, as said below
- gain_first: bfloat16 [768], P(('dp', 'tensor')), may hold values from 0.25 to 1.75
- inlet_weight: bfloat16 [768, 3, 12, 64], P('dp', None, 'tensor'), may hold values from -0.21875 to 0.21875
- outlet_weight: bfloat16 [12, 64, 768], P('tensor', None, 'dp'), may hold values from -0.875 to 0.875
- gain_second: bfloat16 [768], P(('dp', 'tensor')), may hold values from 0.25 to 1.75
- up_weight: bfloat16 [768, 3072], P(None, ('dp', 'tensor')), may hold values from -0.21875 to 0.21875
- up_bias: bfloat16 [3072], P(('dp', 'tensor')), may hold values from -3 to 3
- down_weight: bfloat16 [3072, 768], P(('dp', 'tensor')), may hold values from -0.109375 to 0.109375
- down_bias: bfloat16 [768], P(('dp', 'tensor')), may hold values from -2 to 2
- modulator: bfloat16 [128, 6, 768], P(None, None, ('dp', 'tensor')), may hold values from -0.5 to 0.5
- modulator_bias: bfloat16 [6, 768], P(None, ('dp', 'tensor')), may hold values from -3 to 3
Outputs:
- layer_output: bfloat16 [28672, 768], P(('dp', 'tensor'))
- adjoint_tokens: bfloat16 [28672, 768], P(('dp', 'tensor'))
- adjoint_gain_first: float32 [768], P(('dp', 'tensor'))
- adjoint_inlet: float32 [768, 3, 12, 64], P('dp', None, 'tensor')
- adjoint_outlet: float32 [12, 64, 768], P('tensor', None, 'dp')
- adjoint_gain_second: float32 [768], P(('dp', 'tensor'))
- adjoint_up_weight: float32 [768, 3072], P(None, ('dp', 'tensor'))
- adjoint_up_bias: float32 [3072], P(('dp', 'tensor'))
- adjoint_down_weight: float32 [3072, 768], P(('dp', 'tensor'))
- adjoint_down_bias: float32 [768], P(('dp', 'tensor'))
- adjoint_modulator: float32 [128, 6, 768], P(None, None, ('dp', 'tensor'))
- adjoint_modulator_bias: float32 [6, 768], P(None, ('dp', 'tensor'))
Inputs may be any that keep to these rules, and one draw needn't show every extreme that they name: block_parent[t, b] is the parent block of block b of tree t. Blocks 0 to 1 are the trunk: block 0 is its own parent and block b > 0 has parent b - 1. The next 4 blocks are branches, each with a trunk block as parent; the last 8 blocks are leaves, each with a branch block as parent. positions of a token = 128 times the number of strict ancestors of its block plus its place within its block.
All inputs are finite; a program needn't handle non-finite values.
Results may differ from a plain program's by a relative error of at most 0.02.
The roundings to bfloat16 on the way count: a program that leaves them out, or rounds other values in their place, can miss the bound.
Values may be sent and summed in bfloat16 or wider, within the bound.
No kernel may reach another device: no remote copies, remote signals or barrier semaphores. Data moves between devices by JAX's collectives and lax.ppermute only.
A program may use at most 192 MiB of HBM per device.

v0:
```python
from functools import partial

import jax
import jax.numpy as jnp
from jax import lax
from jax.sharding import PartitionSpec as P

EPS = 1e-05
ROPE_BASE = 10000.0
MASKED = -1e30
HIGHEST = lax.Precision.HIGHEST


def modulate(values, weight_gain, offset, stretch):
    center = values - jnp.mean(values, axis=-1, keepdims=True)
    second = jnp.mean(center * center, axis=-1, keepdims=True)
    return center * lax.rsqrt(second + EPS) * weight_gain * (1.0 + stretch) + offset


def rotary_tables(places, width):
    halfway = width // 2
    inverse = ROPE_BASE ** (-(jnp.arange(halfway, dtype=jnp.float32) * 2.0 / width))
    angles = places.astype(jnp.float32)[:, None] * inverse[None, :]
    return (jnp.cos(angles), jnp.sin(angles))


def rotate(vectors, cosine, sine_part):
    halfway = vectors.shape[-1] // 2
    former = vectors[..., :halfway]
    latter = vectors[..., halfway:]
    cosine = cosine[:, None, :]
    sine_part = sine_part[:, None, :]
    return jnp.concatenate(
        [former * cosine - latter * sine_part, latter * cosine + former * sine_part], axis=-1
    )


def path_mask(parents, length):
    amount = parents.shape[0]
    labels = jnp.arange(amount, dtype=jnp.int32)
    climb_map = (parents[:, None] == labels[None, :]).astype(jnp.float32)
    identity = jnp.eye(amount, dtype=jnp.float32)

    def climb(iteration, carried):
        reached, ancestry = carried
        reached = jnp.dot(reached, climb_map, precision=HIGHEST)
        return (reached, jnp.maximum(ancestry, reached))

    reached, ancestry = lax.fori_loop(0, amount, climb, (identity, identity))
    linked = jnp.maximum(ancestry, ancestry.T)
    owners = jnp.arange(length, dtype=jnp.int32) // (length // amount)
    chooser = (owners[:, None] == labels[None, :]).astype(jnp.float32)
    joined = jnp.dot(jnp.dot(chooser, linked, precision=HIGHEST), chooser.T, precision=HIGHEST)
    return joined > 0.5


def head_order(array):
    return jnp.transpose(array, (1, 0, 2))


def fetch_layer(inlet_weight, outlet_weight, up_weight, down_weight, up_bias):
    return (
        lax.all_gather(inlet_weight, "dp", axis=0, tiled=True),
        lax.all_gather(outlet_weight, "dp", axis=2, tiled=True),
        lax.all_gather(up_weight, "dp", axis=1, tiled=True),
        lax.all_gather(down_weight, "dp", axis=0, tiled=True),
        lax.all_gather(up_bias, "dp", axis=0, tiled=True),
    )


def head_forward(allowed, scale_factor, bundle):
    queries, keys_rot, values_v = bundle
    scores = jnp.dot(queries, keys_rot.T, preferred_element_type=jnp.float32)
    logits = jnp.where(allowed, scores * scale_factor, MASKED)
    highest = jnp.max(logits, axis=-1, keepdims=True)
    raised = jnp.exp(logits - highest)
    totals = jnp.sum(raised, axis=-1, keepdims=True)
    probs = raised / totals
    attended = jnp.dot(probs.astype(jnp.bfloat16), values_v, preferred_element_type=jnp.float32)
    return (attended.astype(jnp.bfloat16), (highest + jnp.log(totals))[:, 0])


def head_backward(allowed, scale_factor, bundle):
    queries, keys_rot, values_v, slope, log_total = bundle
    scores = jnp.dot(queries, keys_rot.T, preferred_element_type=jnp.float32)
    logits = jnp.where(allowed, scores * scale_factor, MASKED)
    probs = jnp.exp(logits - log_total[:, None])
    value_adj = jnp.dot(probs.astype(jnp.bfloat16).T, slope, preferred_element_type=jnp.float32)
    prob_slope = jnp.dot(slope, values_v.T, preferred_element_type=jnp.float32)
    inner = jnp.sum(probs * prob_slope, axis=-1, keepdims=True)
    score_slope = (probs * (prob_slope - inner) * scale_factor).astype(jnp.bfloat16)
    query_adj = jnp.dot(score_slope, keys_rot, preferred_element_type=jnp.float32)
    key_adj = jnp.dot(score_slope.T, queries, preferred_element_type=jnp.float32)
    return (query_adj, key_adj, value_adj)


def per_device(
    tokens,
    cotangent,
    time_embed,
    block_parent,
    positions,
    gain_first,
    inlet_weight,
    outlet_weight,
    gain_second,
    up_weight,
    up_bias,
    down_weight,
    down_bias,
    modulator,
    modulator_bias,
):
    smalls = (
        lax.all_gather(gain_first, ("dp", "tensor"), axis=0, tiled=True),
        lax.all_gather(gain_second, ("dp", "tensor"), axis=0, tiled=True),
        lax.all_gather(down_bias, ("dp", "tensor"), axis=0, tiled=True),
        lax.all_gather(modulator_bias, ("dp", "tensor"), axis=1, tiled=True),
        lax.all_gather(modulator, ("dp", "tensor"), axis=2, tiled=True),
    )
    norm_one, norm_two, bias_down, bias_mod, weight_mod = [
        member.astype(jnp.float32) for member in smalls
    ]
    width = tokens.shape[1]
    inlet_full, outlet_full, up_full, down_full, up_bias_full = fetch_layer(
        inlet_weight, outlet_weight, up_weight, down_weight, up_bias
    )
    local_heads = inlet_full.shape[2]
    head_width = inlet_full.shape[3]
    inlet_flat = inlet_full.reshape(width, -1)
    outlet_flat = outlet_full.reshape(local_heads * head_width, width)
    embed_act = jax.nn.silu(time_embed)
    shifts = (
        jnp.dot(embed_act, weight_mod.reshape(weight_mod.shape[0], -1), precision=HIGHEST).reshape(
            6, width
        )
        + bias_mod
    )
    values = tokens.astype(jnp.float32)
    normed = modulate(values, norm_one, shifts[0], shifts[1]).astype(jnp.bfloat16)
    normed_all = lax.all_gather(normed, "tensor", axis=0, tiled=True)
    length = normed_all.shape[0]
    mixed = jnp.dot(normed_all, inlet_flat, preferred_element_type=jnp.float32).reshape(
        length, 3, local_heads, head_width
    )
    cosine, sine_part = rotary_tables(positions, head_width)
    queries = head_order(rotate(mixed[:, 0], cosine, sine_part).astype(jnp.bfloat16))
    keys_rot = head_order(rotate(mixed[:, 1], cosine, sine_part).astype(jnp.bfloat16))
    values_v = head_order(mixed[:, 2].astype(jnp.bfloat16))
    allowed = path_mask(block_parent[0], length)
    scale_factor = head_width ** (-0.5)
    attended_heads, log_totals = lax.map(
        partial(head_forward, allowed, scale_factor), (queries, keys_rot, values_v)
    )
    attended = head_order(attended_heads).reshape(length, local_heads * head_width)
    branch_part = jnp.dot(attended, outlet_flat, preferred_element_type=jnp.float32)
    branch = lax.psum_scatter(
        branch_part.astype(jnp.bfloat16), "tensor", scatter_dimension=0, tiled=True
    ).astype(jnp.float32)
    middle = values + shifts[2] * branch
    normed_two = modulate(middle, norm_two, shifts[3], shifts[4]).astype(jnp.bfloat16)
    normed_two_all = lax.all_gather(normed_two, "tensor", axis=0, tiled=True)
    hidden = jnp.dot(
        normed_two_all, up_full, preferred_element_type=jnp.float32
    ) + up_bias_full.astype(jnp.float32)
    activated = jax.nn.gelu(hidden, approximate=True).astype(jnp.bfloat16)
    mlp_part = jnp.dot(activated, down_full, preferred_element_type=jnp.float32)
    mlp_out = lax.psum_scatter(
        mlp_part.astype(jnp.bfloat16), "tensor", scatter_dimension=0, tiled=True
    ).astype(jnp.float32)
    layer_output = (middle + shifts[5] * (mlp_out + bias_down)).astype(jnp.bfloat16)
    inlet_full, outlet_full, up_full, down_full, up_bias_full = fetch_layer(
        inlet_weight, outlet_weight, up_weight, down_weight, up_bias
    )
    inlet_flat = inlet_full.reshape(width, -1)
    outlet_flat = outlet_full.reshape(local_heads * head_width, width)
    slope = cotangent.astype(jnp.float32)
    gate_two_adj = jnp.sum(slope * (mlp_out + bias_down), axis=0)
    down_bias_adj = jnp.sum(slope, axis=0) * shifts[5]
    mlp_slope = (slope * shifts[5]).astype(jnp.bfloat16)
    mlp_slope_all = lax.all_gather(mlp_slope, "tensor", axis=0, tiled=True)
    down_adj = jnp.dot(activated.T, mlp_slope_all, preferred_element_type=jnp.float32)
    act_slope = jnp.dot(mlp_slope_all, down_full.T, preferred_element_type=jnp.float32)
    gelu_back = jax.vjp(partial(jax.nn.gelu, approximate=True), hidden)[1]
    hidden_slope = gelu_back(act_slope)[0].astype(jnp.bfloat16)
    up_bias_adj = jnp.sum(hidden_slope.astype(jnp.float32), axis=0)
    up_adj = jnp.dot(normed_two_all.T, hidden_slope, preferred_element_type=jnp.float32)
    norm_two_part = jnp.dot(hidden_slope, up_full.T, preferred_element_type=jnp.float32)
    norm_two_slope = lax.psum_scatter(
        norm_two_part.astype(jnp.bfloat16), "tensor", scatter_dimension=0, tiled=True
    ).astype(jnp.float32)
    middle_back = jax.vjp(modulate, middle, norm_two, shifts[3], shifts[4])[1]
    middle_adj, gain_two_adj, shift_two_adj, scale_two_adj = middle_back(norm_two_slope)
    middle_slope = slope + middle_adj
    gate_one_adj = jnp.sum(middle_slope * branch, axis=0)
    branch_slope = (middle_slope * shifts[2]).astype(jnp.bfloat16)
    branch_slope_all = lax.all_gather(branch_slope, "tensor", axis=0, tiled=True)
    outlet_adj = jnp.dot(attended.T, branch_slope_all, preferred_element_type=jnp.float32)
    attended_slope = jnp.dot(
        branch_slope_all, outlet_flat.T, preferred_element_type=jnp.float32
    ).astype(jnp.bfloat16)
    attended_slope = head_order(attended_slope.reshape(length, local_heads, head_width))
    query_adj, key_adj, value_adj = lax.map(
        partial(head_backward, allowed, scale_factor),
        (queries, keys_rot, values_v, attended_slope, log_totals),
    )
    query_adj = rotate(head_order(query_adj), cosine, -sine_part)
    key_adj = rotate(head_order(key_adj), cosine, -sine_part)
    mixed_slope = (
        jnp.stack([query_adj, key_adj, head_order(value_adj)], axis=1)
        .astype(jnp.bfloat16)
        .reshape(length, -1)
    )
    inlet_adj = jnp.dot(normed_all.T, mixed_slope, preferred_element_type=jnp.float32).reshape(
        width, 3, local_heads, head_width
    )
    normed_part = jnp.dot(mixed_slope, inlet_flat.T, preferred_element_type=jnp.float32)
    normed_slope = lax.psum_scatter(
        normed_part.astype(jnp.bfloat16), "tensor", scatter_dimension=0, tiled=True
    ).astype(jnp.float32)
    values_back = jax.vjp(modulate, values, norm_one, shifts[0], shifts[1])[1]
    values_adj, gain_one_adj, shift_one_adj, scale_one_adj = values_back(normed_slope)
    adjoint_tokens = (middle_slope + values_adj).astype(jnp.bfloat16)
    shift_adj = jnp.stack(
        [shift_one_adj, scale_one_adj, gate_one_adj, shift_two_adj, scale_two_adj, gate_two_adj]
    )
    mod_weight_adj = embed_act[0][:, None, None] * shift_adj[None]
    outlet_adj = outlet_adj.reshape(local_heads, head_width, width)
    inlet_share, outlet_share, up_share, down_share, up_bias_share = (
        lax.psum_scatter(inlet_adj, "dp", scatter_dimension=0, tiled=True),
        lax.psum_scatter(outlet_adj, "dp", scatter_dimension=2, tiled=True),
        lax.psum_scatter(up_adj, "dp", scatter_dimension=1, tiled=True),
        lax.psum_scatter(down_adj, "dp", scatter_dimension=0, tiled=True),
        lax.psum_scatter(up_bias_adj, "dp", scatter_dimension=0, tiled=True),
    )
    gain_one_share, gain_two_share, down_bias_share, mod_bias_share, mod_weight_share = (
        lax.psum_scatter(gain_one_adj, ("dp", "tensor"), scatter_dimension=0, tiled=True),
        lax.psum_scatter(gain_two_adj, ("dp", "tensor"), scatter_dimension=0, tiled=True),
        lax.psum_scatter(down_bias_adj, ("dp", "tensor"), scatter_dimension=0, tiled=True),
        lax.psum_scatter(shift_adj, ("dp", "tensor"), scatter_dimension=1, tiled=True),
        lax.psum_scatter(mod_weight_adj, ("dp", "tensor"), scatter_dimension=2, tiled=True),
    )
    return (
        layer_output,
        adjoint_tokens,
        gain_one_share,
        inlet_share,
        outlet_share,
        gain_two_share,
        up_share,
        up_bias_share,
        down_share,
        down_bias_share,
        mod_weight_share,
        mod_bias_share,
    )


def solution(mesh):
    in_specs = (
        P(("dp", "tensor"), None),
        P(("dp", "tensor"), None),
        P("dp", None),
        P("dp", None),
        P("dp"),
        P(("dp", "tensor")),
        P("dp", None, "tensor", None),
        P("tensor", None, "dp"),
        P(("dp", "tensor")),
        P(None, ("dp", "tensor")),
        P(("dp", "tensor")),
        P(("dp", "tensor"), None),
        P(("dp", "tensor")),
        P(None, None, ("dp", "tensor")),
        P(None, ("dp", "tensor")),
    )
    out_specs = (
        P(("dp", "tensor"), None),
        P(("dp", "tensor"), None),
        P(("dp", "tensor")),
        P("dp", None, "tensor", None),
        P("tensor", None, "dp"),
        P(("dp", "tensor")),
        P(None, ("dp", "tensor")),
        P(("dp", "tensor")),
        P(("dp", "tensor"), None),
        P(("dp", "tensor")),
        P(None, None, ("dp", "tensor")),
        P(None, ("dp", "tensor")),
    )
    return jax.shard_map(
        per_device, mesh=mesh, in_specs=in_specs, out_specs=out_specs, check_vma=False
    )
```

profile of v0, /device:TPU:0, one launch (start us, length us, event | category | flops | bytes accessed | tf_op | source)
XLA Modules:
  0.0 1269.5 jit_solution(4032610746774366570)
XLA Ops:
  11.3 42.1 %all-reduce.10 = (bf16[768]{0:T(1024)(128)(2,1)}, bf16[768]{0:T(1024)(128)(2,1)S(1)}, bf16[768]{0:T(1024)(128)(2,1)}) all-reduce(bf16[768]{0:T(1024)(128)(2,1)S(1)} %dynamic-update-slice.1, bf16[768]{0:T(1024)(128)(2,1)S(1)} %dynamic-update-slice, ...), channel_id=1, replica_groups=mesh['dp'=16,'tensor'=2] {'dp','tensor'}, use_global_device_ids=true, to_apply=%add.1 | all-reduce | flops 2304 | bytes 9216
  53.4 67.6 %all-gather = bf16[32,24,6]{1,2,0:T(8,128)(2,1)S(1)} all-gather(bf16[1,24,6]{1,2,0:T(8,128)(2,1)} %bitcast.206), channel_id=1, replica_groups=mesh['dp'=16,'tensor'=2] {'dp','tensor'}, dimensions={0}, use_global_device_ids=true | all-gather | bytes 9504 | tf_op jit(solution)/shard_map/all_gather | solution.py:118
  132.6 7.7 convolution_compare_fusion
  143.7 22.4 %all_gather.51 = bf16[6,64,768]{1,2,0:T(8,128)(2,1)} all-gather(bf16[6,64,48]{1,2,0:T(8,128)(2,1)S(1)} %copy-done.23), channel_id=1, replica_groups=mesh['dp'=16,'tensor'=2] {'dp'}, dimensions={2}, use_global_device_ids=true | all-gather | bytes 626688 | tf_op jit(solution)/shard_map/all_gather | solution.py:64
  167.8 4.7 copy.71
  172.6 5.7 fusion.83
  190.9 4.0 copy.74
  194.9 59.2 %while.39 = (s32[]{:T(128)}, bf16[6,1792,64]{1,2,0:T(8,128)(2,1)}, f32[6,1792]{1,0:T(8,128)S(1)}, bf16[6,1792,64]{2,1,0:T(8,128)(2,1)}, bf16[6,1792,64]{2,1,0:T(...) while((s32[]{:T(128)}, bf16[6,1792,64]{1,2,0:T(8,128)(2,1)}, ...), condition=%wide.region_7.8_spmd, body=%wide.region_4.7_spmd.sunk | while | flops 847886592 | bytes 43440232 | solution.py:152
  200.3 4.2 fusion.157
  210.2 4.2 fusion.157
  220.1 4.2 fusion.157
  229.9 4.2 fusion.157
  239.8 4.2 fusion.157
  249.7 4.2 fusion.157
  254.1 5.6 bitcast_convert_fusion.1
  260.7 35.5 %reduce-scatter.11.cloned.1.call-done = bf16[896,768]{1,0:T(8,128)(2,1)} async-done(((bf16[1792,768]{1,0:T(8,128)(2,1)}), bf16[896,768]{1,0:T(8,128)(2,1)}) %reduce-scatter.11.cloned.1.call-update) | async-done | bytes 1376272 | tf_op jit(solution)/shard_map/reduce_scatter | solution.py:157
  306.7 33.3 %all-reduce.2 = bf16[1536]{0:T(1024)(128)(2,1)S(1)} all-reduce(bf16[1536]{0:T(1024)(128)(2,1)S(1)} %dynamic-update-slice.2), channel_id=1, replica_groups=mesh['dp'=16,'tensor'=2] {'dp'}, use_global_device_ids=true, to_apply=%add.2 | all-reduce | flops 1536 | bytes 6144
  340.8 41.2 %all-gather.16.cloned.1.call-done = bf16[1792,768]{1,0:T(8,128)(2,1)} async-done(((bf16[896,768]{1,0:T(8,128)(2,1)}), bf16[1792,768]{1,0:T(8,128)(2,1)}) %all-gather.16.cloned.1.call-update) | async-done | bytes 2752528 | tf_op jit(solution)/shard_map/all_gather | solution.py:162
  382.0 12.3 multiply_convert_fusion.1
  394.2 32.4 %all-gather.20.cloned.1.call-done = bf16[1536,768]{1,0:T(8,128)(2,1)} async-done(((bf16[96,768]{1,0:T(8,128)(2,1)}), bf16[1536,768]{1,0:T(8,128)(2,1)}) %all-gather.20.cloned.1.call-update) | async-done | bytes 2359312 | tf_op jit(solution)/shard_map/all_gather | solution.py:66
  426.6 40.8 %all-gather.22.cloned.1.call-done = bf16[1792,768]{1,0:T(8,128)(2,1)} async-done(((bf16[896,768]{1,0:T(8,128)(2,1)}), bf16[1792,768]{1,0:T(8,128)(2,1)}) %all-gather.22.cloned.1.call-update) | async-done | bytes 2752528 | tf_op jit(solution)/shard_map/all_gather | solution.py:181
  467.4 15.4 %convert_reduce_fusion = (f32[1536]{0:T(1024)}, bf16[1792,1536]{1,0:T(8,128)(2,1)S(1)}) fusion(f32[1792,1536]{1,0:T(8,128)} %get-tuple-element.307, f32[1536]{0:T(1024)S(1)} %convert_element_type.125, bf16[1792,768]{1,0:T(8,128)(2,1)} %all-gather.22.cloned.1.call-done, bf16[1536,768]{1,0:T(8,128)(2,1)} %all-gather.20.cloned.1.call-done), kind=kOutput, calls=%fused_computation.63 | convolution fusion | flops 4291164672 | bytes 21639168 | tf_op jit(solution)/shard_map/dot_general | solution.py:183
  485.1 5.7 convolution_convert_fusion
  491.3 9.3 convolution_convert_fusion.1
  501.2 28.8 %reduce-scatter.15.cloned.1.call-done = bf16[896,768]{1,0:T(8,128)(2,1)} async-done(((bf16[1792,768]{1,0:T(8,128)(2,1)}), bf16[896,768]{1,0:T(8,128)(2,1)}) %reduce-scatter.15.cloned.1.call-update) | async-done | bytes 1376272 | tf_op jit(solution)/shard_map/reduce_scatter | solution.py:189
  536.2 35.1 %reduce-scatter.13.cloned.1.call-done = bf16[896,768]{1,0:T(8,128)(2,1)} async-done(((bf16[1792,768]{1,0:T(8,128)(2,1)}), bf16[896,768]{1,0:T(8,128)(2,1)}) %reduce-scatter.13.cloned.1.call-update) | async-done | bytes 1376272 | tf_op jit(solution)/shard_map/reduce_scatter | solution.py:168
  571.3 6.1 fusion.75
  582.8 38.2 %all-gather.24.cloned.1.call-done = bf16[1792,768]{1,0:T(8,128)(2,1)} async-done(((bf16[896,768]{1,0:T(8,128)(2,1)}), bf16[1792,768]{1,0:T(8,128)(2,1)}) %all-gather.24.cloned.1.call-update) | async-done | bytes 2752528 | tf_op jit(solution)/shard_map/all_gather | solution.py:197
  621.0 4.3 convolution_convert_fusion.2
  629.1 154.9 %while.40 = (s32[]{:T(128)}, f32[6,1792,64]{1,2,0:T(8,128)}, f32[6,1792,64]{1,2,0:T(8,128)}, bf16[6,1792,64]{1,2,0:T(8,128)(2,1)}, bf16[6,1792,64]{2,1,0:T(8,128...) while((s32[]{:T(128)}, f32[6,1792,64]{1,2,0:T(8,128)}, ...), condition=%wide.region_17.18_spmd, body=%wide.region_15.17_spmd.sunk | while | flops 2087319808 | bytes 155558096 | solution.py:203
  633.8 6.2 multiply_reduce_fusion.3
  659.6 6.2 multiply_reduce_fusion.3
  685.4 6.2 multiply_reduce_fusion.3
  711.2 6.2 multiply_reduce_fusion.3
  737.0 6.2 multiply_reduce_fusion.3
  747.1 4.0 fusion.169
  762.9 6.2 multiply_reduce_fusion.3
  789.9 8.3 bitcast_convert_fusion
  798.3 10.0 fusion.114
  808.4 10.1 fusion.115
  818.8 6.0 fusion.85
  824.9 10.4 fusion.55
  844.2 33.7 %all-reduce.6 = f32[1536]{0:T(1024)S(1)} all-reduce(f32[1536]{0:T(1024)S(1)} %copy-done.38), channel_id=11, replica_groups=mesh['dp'=16,'tensor'=2] {'dp'}, use_global_device_ids=true, to_apply=%region_29.30.clone | all-reduce | flops 1536 | bytes 12288
  878.6 39.2 %all-reduce.9 = (f32[768]{0:T(1024)S(1)}, f32[768]{0:T(1024)S(1)}, f32[768]{0:T(1024)S(1)}, f32[6,768]{1,0:T(8,128)S(1)}) all-reduce(f32[768]{0:T(1024)S(1)} %get-tuple-element.216, f32[768]{0:T(1024)S(1)} %copy-done.33, f32[768]{0:T(1024)S(1)} %mul.488, ...), channel_id=6, replica_groups=mesh['dp'=16,'tensor'=2] {'dp','tensor'}, use_global_device_ids=true, to_apply=%region_22.23.clone | all-reduce | flops 6912 | bytes 55296
  923.7 73.9 %reduce-scatter.25.cloned.1.call-done = f32[96,768]{1,0:T(8,128)} async-done(((f32[1536,768]{1,0:T(8,128)}), f32[96,768]{1,0:T(8,128)}) %reduce-scatter.25.cloned.1.call-update) | async-done | bytes 294928 | tf_op jit(solution)/shard_map/reduce_scatter | solution.py:233
  997.6 66.6 %reduce-scatter.21.cloned.1.call-done = f32[6,64,48]{1,2,0:T(8,128)} async-done(((f32[6,64,768]{1,2,0:T(8,128)}), f32[6,64,48]{1,2,0:T(8,128)}) %reduce-scatter.21.cloned.1.call-update) | async-done | bytes 73744 | tf_op jit(solution)/shard_map/reduce_scatter | solution.py:231
  1064.2 93.3 %reduce-scatter.19.cloned.1.call-done = f32[48,3,6,64]{3,0,2,1:T(8,128)} async-done(((f32[768,3,6,64]{3,0,2,1:T(8,128)}), f32[48,3,6,64]{3,0,2,1:T(8,128)}) %reduce-scatter.19.cloned.1.call-update) | async-done | bytes 221200 | tf_op jit(solution)/shard_map/reduce_scatter | solution.py:230
  1157.5 105.0 %reduce-scatter.27.cloned.1.call-done = f32[128,6,24]{0,2,1:T(8,128)} async-done(((f32[128,6,768]{0,2,1:T(8,128)}), f32[128,6,24]{0,2,1:T(8,128)}) %reduce-scatter.27.cloned.1.call-update) | async-done | bytes 73744 | tf_op jit(solution)/shard_map/reduce_scatter | solution.py:241
  (342 shorter events, 234.5 us)
Async XLA Ops:
  7.2 115.8 %copy-start.3 = (bf16[896,768]{1,0:T(8,128)(2,1)S(1)}, bf16[896,768]{1,0:T(8,128)(2,1)}, u32[]{:S(2)}) copy-start(bf16[896,768]{1,0:T(8,128)(2,1)} %param.21) | copy-start | bytes 4128772
  7.2 116.4 %copy-start.42 = (f32[1,128]{1,0:T(1,128)S(1)}, f32[1,128]{1,0:T(1,128)}, u32[]{:S(2)}) copy-start(f32[1,128]{1,0:T(1,128)} %param.23) | copy-start | bytes 1540
  7.2 116.4 %all-gather.10.cloned.1.call-start = ((), (), s32[]{:S(2)}) async-start(), calls=%async_computation.9 | async-start | bytes 1216512 | tf_op jit(solution)/shard_map/all_gather | solution.py:119
  7.9 159.9 %all-gather.14.cloned.1.call-start = ((), (), s32[]{:S(2)}) async-start(), calls=%async_computation.11 | async-start | bytes 3760128 | tf_op jit(solution)/shard_map/all_gather | solution.py:63
  8.7 163.9 %all-gather.12.cloned.1.call-start = ((), (), s32[]{:S(2)}) async-start(), calls=%async_computation.10 | async-start | bytes 4128768 | tf_op jit(solution)/shard_map/all_gather | solution.py:141
  53.4 74.9 %copy-start.18 = (f32[768]{0:T(1024)}, f32[768]{0:T(1024)S(1)}, u32[]{:S(2)}) copy-start(f32[768]{0:T(1024)S(1)} %convert_element_type.115) | copy-start | bytes 9220
  123.0 5.3 copy-start.16
  123.5 5.3 copy-start.28
  123.5 5.3 copy-start.46
  123.5 5.3 copy-start.26
  123.5 8.4 copy-start.37
  126.5 6.1 copy-start.20
  128.3 167.9 %reduce-scatter.11.cloned.1.call-start = ((), (), s32[]{:S(2)}) async-start(), calls=%async_computation.12 | async-start | bytes 4128768 | tf_op jit(solution)/shard_map/reduce_scatter | solution.py:157
  140.3 3.4 copy-start.23
  167.8 12.1 copy-start.13
  259.8 36.4 %copy-start.15 = (f32[768]{0:T(1024)S(1)}, f32[768]{0:T(1024)}, u32[]{:S(2)}) copy-start(f32[768]{0:T(1024)} %get-tuple-element.226) | copy-start | bytes 9220
  259.8 81.0 %all-gather.18.cloned.1.call-start = ((), (), s32[]{:S(2)}) async-start(), calls=%async_computation.14 | async-start | bytes 2506752 | tf_op jit(solution)/shard_map/all_gather | solution.py:65
  260.4 121.6 %all-gather.16.cloned.1.call-start = ((), (), s32[]{:S(2)}) async-start(), calls=%async_computation.13 | async-start | bytes 4128768 | tf_op jit(solution)/shard_map/all_gather | solution.py:162
  296.2 3.4 copy-start.22
  296.2 3.4 copy-start.36
  301.5 3.6 copy-start.41
  301.5 4.9 copy-start.47
  301.6 125.0 %all-gather.20.cloned.1.call-start = ((), (), s32[]{:S(2)}) async-start(), calls=%async_computation.15 | async-start | bytes 2506752 | tf_op jit(solution)/shard_map/all_gather | solution.py:66
  302.3 165.0 %all-gather.22.cloned.1.call-start = ((), (), s32[]{:S(2)}) async-start(), calls=%async_computation.17 | async-start | bytes 4128768 | tf_op jit(solution)/shard_map/all_gather | solution.py:181
  305.1 225.0 %reduce-scatter.15.cloned.1.call-start = ((), (), s32[]{:S(2)}) async-start(), calls=%async_computation.18 | async-start | bytes 4128768 | tf_op jit(solution)/shard_map/reduce_scatter | solution.py:189
  467.4 17.8 %copy-start.44 = (bf16[768,1536]{0,1:T(8,128)(2,1)S(1)}, bf16[768,1536]{0,1:T(8,128)(2,1)}, u32[]{:S(2)}) copy-start(bf16[768,1536]{0,1:T(8,128)(2,1)} %all-gather.18.cloned.1.call-done) | copy-start | bytes 7077892
  490.8 80.5 %reduce-scatter.13.cloned.1.call-start = ((), (), s32[]{:S(2)}) async-start(), calls=%async_computation.16 | async-start | bytes 4128768 | tf_op jit(solution)/shard_map/reduce_scatter | solution.py:168
  500.6 120.4 %all-gather.24.cloned.1.call-start = ((), (), s32[]{:S(2)}) async-start(), calls=%async_computation.19 | async-start | bytes 4128768 | tf_op jit(solution)/shard_map/all_gather | solution.py:197
  530.1 3.4 copy-start.5
  530.1 3.4 copy-start.8
  530.1 3.4 copy-start.11
  580.4 257.2 %reduce-scatter.17.cloned.1.call-start = ((), (), s32[]{:S(2)}) async-start(), calls=%async_computation.20 | async-start | bytes 4128768 | tf_op jit(solution)/shard_map/reduce_scatter | solution.py:218
  643.9 3.9 copy-start
  669.6 4.0 copy-start
  695.5 4.0 copy-start
  721.3 3.9 copy-start
  747.1 4.0 copy-start
  772.9 4.0 copy-start
  798.3 125.4 %reduce-scatter.23.cloned.1.call-start = ((), (), s32[]{:S(2)}) async-start(), calls=%async_computation.23 | async-start | bytes 5013504 | tf_op jit(solution)/shard_map/reduce_scatter | solution.py:232
  808.4 189.2 %reduce-scatter.25.cloned.1.call-start = ((), (), s32[]{:S(2)}) async-start(), calls=%async_computation.24 | async-start | bytes 5013504 | tf_op jit(solution)/shard_map/reduce_scatter | solution.py:233
  818.5 245.7 %reduce-scatter.21.cloned.1.call-start = ((), (), s32[]{:S(2)}) async-start(), calls=%async_computation.22 | async-start | bytes 2506752 | tf_op jit(solution)/shard_map/reduce_scatter | solution.py:231
  824.8 332.7 %reduce-scatter.19.cloned.1.call-start = ((), (), s32[]{:S(2)}) async-start(), calls=%async_computation.21 | async-start | bytes 7520256 | tf_op jit(solution)/shard_map/reduce_scatter | solution.py:230
  835.4 4.4 copy-start.29
  835.4 4.4 copy-start.27
  835.4 427.1 %reduce-scatter.27.cloned.1.call-start = ((), (), s32[]{:S(2)}) async-start(), calls=%async_computation.25 | async-start | bytes 2433024 | tf_op jit(solution)/shard_map/reduce_scatter | solution.py:241
  841.6 36.9 %copy-start.25 = (f32[768]{0:T(1024)S(1)}, f32[768]{0:T(1024)}, u32[]{:S(2)}) copy-start(f32[768]{0:T(1024)} %get-tuple-element.221) | copy-start | bytes 9220
  841.6 36.9 %copy-start.30 = (f32[768]{0:T(1024)S(1)}, f32[768]{0:T(1024)}, u32[]{:S(2)}) copy-start(f32[768]{0:T(1024)} %get-tuple-element.295) | copy-start | bytes 9220
  841.6 36.9 %copy-start.33 = (f32[768]{0:T(1024)S(1)}, f32[768]{0:T(1024)}, u32[]{:S(2)}) copy-start(f32[768]{0:T(1024)} %get-tuple-element.213) | copy-start | bytes 9220
  (33 other events, 65.1 us)
Sparse Core Ops, SparseCore 0:
  10.9 54.4 all-gather.9
  67.6 47.3 all-gather.13
  128.4 36.3 all-gather.11
  259.9 36.2 reduce-scatter.10
  298.3 42.4 all-gather.17
  342.8 39.1 all-gather.15
  384.2 42.3 all-gather.19
  428.1 39.1 all-gather.21
  490.9 39.0 reduce-scatter.14
  532.2 39.0 reduce-scatter.12
  580.5 40.4 all-gather.23
  798.4 39.0 reduce-scatter.16
  841.9 76.5 reduce-scatter.22
  922.8 74.7 reduce-scatter.24
  1001.7 62.4 reduce-scatter.20
  1068.6 88.8 reduce-scatter.18
  1163.2 99.2 reduce-scatter.26
where the time goes:
time: 1270 us
  waiting for transfers between devices  596 us (47%)
  matrix products  285 us (22%)
  blocking collectives  238 us (19%)
  other arithmetic  77.1 us (6%)
  local copies, waits for them, and re-layouts  54 us (4%)
  between operations  16.4 us (1%)
    unnamed x4, blocking collectives  148 us
    reduce_scatter x1, waiting for transfers between devices, per_device(): lax.psum_scatter(mod_weight_adj, ('dp', 'tensor'), scatter_dimension=2, t...  105 us
    reduce_scatter x1, waiting for transfers between devices, per_device(): lax.psum_scatter(inlet_adj, 'dp', scatter_dimension=0, tiled=True)  93.3 us
    reduce_scatter x1, waiting for transfers between devices, per_device(): lax.psum_scatter(down_adj, 'dp', scatter_dimension=0, tiled=True)  73.9 us
    all_gather x1, blocking collectives, per_device(): lax.all_gather(modulator_bias, ('dp', 'tensor'), axis=1, tiled=True)  67.6 us
    reduce_scatter x1, waiting for transfers between devices, per_device(): lax.psum_scatter(outlet_adj, 'dp', scatter_dimension=2, tiled=True)  66.6 us
    all_gather x1, waiting for transfers between devices, per_device(): normed_two_all = lax.all_gather(normed_two, 'tensor', axis=0, tiled=True)  41.2 us
    all_gather x1, waiting for transfers between devices, per_device(): mlp_slope_all = lax.all_gather(mlp_slope, 'tensor', axis=0, tiled=True)  40.8 us
  transfers between devices with their start and end apart: 17, of which 13 were waited for; matrix products, arithmetic and copies ran while one was open for 9% of the time, Pallas kernels for 0%

commit v1 on v0

v1 whole, which is shorter than its diff:
```python
from functools import partial

import jax
import jax.numpy as jnp
from jax import lax
from jax.sharding import Mesh, PartitionSpec as P

EPS = 1e-05
ROPE_BASE = 10000.0
MASKED = -1e30
HIGHEST = lax.Precision.HIGHEST


def modulate(values, weight_gain, offset, stretch):
    center = values - jnp.mean(values, axis=-1, keepdims=True)
    second = jnp.mean(center * center, axis=-1, keepdims=True)
    return center * lax.rsqrt(second + EPS) * weight_gain * (1.0 + stretch) + offset


def rotary_tables(places, width):
    halfway = width // 2
    inverse = ROPE_BASE ** (-(jnp.arange(halfway, dtype=jnp.float32) * 2.0 / width))
    angles = places.astype(jnp.float32)[:, None] * inverse[None, :]
    return (jnp.cos(angles), jnp.sin(angles))


def rotate(vectors, cosine, sine_part):
    halfway = vectors.shape[-1] // 2
    former = vectors[..., :halfway]
    latter = vectors[..., halfway:]
    cosine = cosine[:, None, :]
    sine_part = sine_part[:, None, :]
    return jnp.concatenate(
        [former * cosine - latter * sine_part, latter * cosine + former * sine_part], axis=-1
    )


def family(climb_map, labels):
    amount = climb_map.shape[0]
    proper = climb_map * (labels[:, None] != labels[None, :])
    reached = proper
    ancestry = proper
    for _ in range(2):
        reached = jnp.dot(reached, proper, precision=HIGHEST)
        ancestry = ancestry + reached
    depth = jnp.sum(ancestry, axis=1)
    return depth, ancestry + ancestry.T + jnp.eye(amount, dtype=jnp.float32)


def head_order(array):
    return jnp.transpose(array, (1, 0, 2))


def head_forward(allowed, scale_factor, bundle):
    queries, keys_rot, values_v = bundle
    scores = jnp.dot(queries, keys_rot.T, preferred_element_type=jnp.float32)
    logits = jnp.where(allowed, scores * scale_factor, MASKED)
    highest = jnp.max(logits, axis=-1, keepdims=True)
    raised = jnp.exp(logits - highest)
    totals = jnp.sum(raised, axis=-1, keepdims=True)
    probs = raised / totals
    attended = jnp.dot(probs.astype(jnp.bfloat16), values_v, preferred_element_type=jnp.float32)
    return (attended.astype(jnp.bfloat16), (highest + jnp.log(totals))[:, 0])


def head_backward(allowed, scale_factor, bundle):
    queries, keys_rot, values_v, slope, log_total = bundle
    scores = jnp.dot(queries, keys_rot.T, preferred_element_type=jnp.float32)
    logits = jnp.where(allowed, scores * scale_factor, MASKED)
    probs = jnp.exp(logits - log_total[:, None])
    value_adj = jnp.dot(probs.astype(jnp.bfloat16).T, slope, preferred_element_type=jnp.float32)
    prob_slope = jnp.dot(slope, values_v.T, preferred_element_type=jnp.float32)
    inner = jnp.sum(probs * prob_slope, axis=-1, keepdims=True)
    score_slope = (probs * (prob_slope - inner) * scale_factor).astype(jnp.bfloat16)
    query_adj = jnp.dot(score_slope, keys_rot, preferred_element_type=jnp.float32)
    key_adj = jnp.dot(score_slope.T, queries, preferred_element_type=jnp.float32)
    return (query_adj, key_adj, value_adj)


ALL = ("chip", "core", "tensor")
CROSS = ("core", "tensor")
DIAGONAL = [(0, 0), (1, 2), (2, 1), (3, 3)]
TURN = [(1, 0), (0, 2), (2, 3), (3, 1)]
TURN_BACK = [(0, 1), (2, 0), (3, 2), (1, 3)]


def diagonal(array):
    return lax.ppermute(array, CROSS, DIAGONAL)


def other_core(array):
    return lax.ppermute(array, "core", [(0, 1), (1, 0)])


def chip_masks(chips):
    masks = []
    mask = chips // 2
    while mask:
        masks.append(mask)
        mask //= 2
    return masks


def partner(array, mask, chips):
    return lax.ppermute(array, "chip", [(i, i ^ mask) for i in range(chips)])


def gather_shards(shard, chips):
    held = jnp.stack([diagonal(shard), lax.ppermute(shard, CROSS, TURN_BACK)])
    for mask in chip_masks(chips):
        held = jnp.concatenate([held, partner(held, mask, chips)], axis=0)
    return held


def scatter_shards(blocks, chips, on_diagonal):
    low = jnp.bfloat16
    for mask in reversed(chip_masks(chips)):
        half = blocks.shape[0] // 2
        arrived = partner(blocks[half:].astype(low), mask, chips)
        blocks = blocks[:half] + arrived.astype(jnp.float32)
    mine, turned = blocks[0], blocks[1]
    straight = diagonal(mine.astype(low)).astype(jnp.float32)
    arrived = lax.ppermute(turned.astype(low), CROSS, TURN).astype(jnp.float32)
    return jnp.where(on_diagonal, mine, straight) + arrived


def block_owners(chips):
    places = [0, 1]
    for mask in chip_masks(chips):
        places = places + [place ^ (2 * mask) for place in places]
    return places


def exchange_small(rows):
    return lax.all_to_all(rows, ALL, split_axis=0, concat_axis=0, tiled=True)


def per_device(
    chips,
    tokens,
    cotangent,
    time_embed,
    block_parent,
    positions,
    gain_first,
    inlet_weight,
    outlet_weight,
    gain_second,
    up_weight,
    up_bias,
    down_weight,
    down_bias,
    modulator,
    modulator_bias,
):
    f32 = jnp.float32
    low = jnp.bfloat16
    devices = chips * 4
    trees = chips * 2
    own_rows, width = tokens.shape
    slim = gain_first.shape[0]
    units = up_bias.shape[0]
    local_heads = inlet_weight.shape[2]
    head_width = inlet_weight.shape[3]
    core = lax.axis_index("core")
    side = lax.axis_index("tensor")
    on_diagonal = core == side
    me = lax.axis_index("chip") * 2 + side
    order = block_owners(chips)
    owners = me ^ jnp.array(order, dtype=jnp.int32)
    spots = jnp.take(
        jnp.array([order.index(i) for i in range(trees)], dtype=jnp.int32),
        me ^ jnp.arange(trees, dtype=jnp.int32),
    )

    small = jnp.concatenate([time_embed[0], block_parent[0].astype(f32)])
    amount = block_parent.shape[1]
    every_embed = exchange_small(
        jnp.broadcast_to(small[None, :], (devices, small.shape[0]))
    ).reshape(trees, 2, -1)[:, 0]
    embeds = every_embed[:, : time_embed.shape[1]]
    tree_row = lax.dynamic_index_in_dim(every_embed, me, 0, keepdims=False)
    parents = tree_row[time_embed.shape[1] :].astype(jnp.int32)
    embeds_act = jax.nn.silu(embeds)
    slices = jnp.dot(
        embeds_act, modulator.astype(f32).reshape(modulator.shape[0], -1), precision=HIGHEST
    ) + modulator_bias.astype(f32).reshape(1, -1)
    slices = jnp.broadcast_to(
        slices.reshape(chips, 1, 2, 6 * slim), (chips, 2, 2, 6 * slim)
    ).reshape(devices, 6 * slim)
    vectors = jnp.concatenate([gain_first, gain_second, down_bias, up_bias]).astype(f32)
    arrived = exchange_small(
        jnp.concatenate(
            [slices, jnp.broadcast_to(vectors[None, :], (devices, vectors.shape[0]))], axis=1
        )
    )
    shifts = (
        arrived[:, : 6 * slim].reshape(devices, 6, slim).transpose(1, 0, 2).reshape(6, width)
    )
    norm_one = arrived[:, 6 * slim : 7 * slim].reshape(width)
    norm_two = arrived[:, 7 * slim : 8 * slim].reshape(width)
    bias_down = arrived[:, 8 * slim : 9 * slim].reshape(width)
    bias_rows = lax.dynamic_index_in_dim(
        arrived[:, 9 * slim :].reshape(trees, 2, units), core, 1, keepdims=False
    )
    up_bias_full = jnp.take(bias_rows, owners, axis=0).reshape(-1)

    inlet_rel = gather_shards(inlet_weight.reshape(inlet_weight.shape[0], -1), chips)
    inlet_flat = jnp.take(inlet_rel, spots, axis=0).reshape(width, -1)
    outlet_rel = gather_shards(outlet_weight.reshape(-1, outlet_weight.shape[2]).T, chips)
    outlet_turned = jnp.take(outlet_rel, spots, axis=0).reshape(width, -1)
    up_turned = gather_shards(up_weight.T, chips).reshape(-1, width)
    down_full = gather_shards(down_weight, chips).reshape(-1, width)

    values = diagonal(tokens).astype(f32)
    slope = diagonal(cotangent).astype(f32)

    def both(array):
        return jnp.concatenate([array, other_core(array)], axis=0)

    def shared(part):
        return part[:own_rows] + other_core(part[own_rows:].astype(low)).astype(f32)

    normed = modulate(values, norm_one, shifts[0], shifts[1]).astype(low)
    normed_all = both(normed)
    length = normed_all.shape[0]
    mixed = jnp.dot(normed_all, inlet_flat, preferred_element_type=f32).reshape(
        length, 3, local_heads, head_width
    )
    labels = jnp.arange(amount, dtype=jnp.int32)
    climb_map = (parents[:, None] == labels[None, :]).astype(f32)
    block_rows = (labels + core * (amount // 2)) % amount
    depth, linked = family(climb_map, labels)
    block = length // amount
    depth_rows = jnp.take(depth, block_rows)
    places = (depth_rows[:, None] * block + jnp.arange(block, dtype=f32)[None, :]).reshape(-1)
    cosine, sine_part = rotary_tables(places, head_width)
    queries = head_order(rotate(mixed[:, 0], cosine, sine_part).astype(low))
    keys_rot = head_order(rotate(mixed[:, 1], cosine, sine_part).astype(low))
    values_v = head_order(mixed[:, 2].astype(low))
    linked = jnp.take(jnp.take(linked, block_rows, axis=0), block_rows, axis=1)
    allowed = jnp.repeat(jnp.repeat(linked > 0.5, block, axis=0), block, axis=1)
    scale_factor = head_width ** (-0.5)
    attended_heads, log_totals = lax.map(
        partial(head_forward, allowed, scale_factor), (queries, keys_rot, values_v)
    )
    attended = head_order(attended_heads).reshape(length, local_heads * head_width)
    branch = shared(
        lax.dot_general(
            attended, outlet_turned, (((1,), (1,)), ((), ())), preferred_element_type=f32
        )
    )
    middle = values + shifts[2] * branch
    normed_two = modulate(middle, norm_two, shifts[3], shifts[4]).astype(low)
    normed_two_all = both(normed_two)
    hidden = (
        lax.dot_general(
            normed_two_all, up_turned, (((1,), (1,)), ((), ())), preferred_element_type=f32
        )
        + up_bias_full
    )
    activated = jax.nn.gelu(hidden, approximate=True).astype(low)
    mlp_out = shared(jnp.dot(activated, down_full, preferred_element_type=f32))
    layer_output = diagonal((middle + shifts[5] * (mlp_out + bias_down)).astype(low))

    gate_two_adj = jnp.sum(slope * (mlp_out + bias_down), axis=0)
    down_bias_adj = jnp.sum(slope, axis=0) * shifts[5]
    mlp_slope_all = both((slope * shifts[5]).astype(low))
    act_slope = lax.dot_general(
        mlp_slope_all, down_full, (((1,), (1,)), ((), ())), preferred_element_type=f32
    )
    down_adj = lax.dot_general(
        activated, mlp_slope_all, (((0,), (0,)), ((), ())), preferred_element_type=f32
    )
    down_share = scatter_shards(down_adj.reshape(trees, -1, width), chips, on_diagonal)
    gelu_back = jax.vjp(partial(jax.nn.gelu, approximate=True), hidden)[1]
    hidden_slope = gelu_back(act_slope)[0].astype(low)
    up_bias_adj = jnp.sum(hidden_slope.astype(f32), axis=0)
    norm_two_part = jnp.dot(hidden_slope, up_turned, preferred_element_type=f32)
    up_adj = lax.dot_general(
        hidden_slope, normed_two_all, (((0,), (0,)), ((), ())), preferred_element_type=f32
    )
    up_share = scatter_shards(up_adj.reshape(trees, -1, width), chips, on_diagonal).T
    norm_two_slope = shared(norm_two_part)
    middle_back = jax.vjp(modulate, middle, norm_two, shifts[3], shifts[4])[1]
    middle_adj, gain_two_adj, shift_two_adj, scale_two_adj = middle_back(norm_two_slope)
    middle_slope = slope + middle_adj
    gate_one_adj = jnp.sum(middle_slope * branch, axis=0)
    branch_slope_all = both((middle_slope * shifts[2]).astype(low))
    attended_slope = jnp.dot(
        branch_slope_all, outlet_turned, preferred_element_type=f32
    ).astype(low)
    outlet_adj = lax.dot_general(
        branch_slope_all, attended, (((0,), (0,)), ((), ())), preferred_element_type=f32
    )
    outlet_share = scatter_shards(
        jnp.take(outlet_adj.reshape(trees, -1, outlet_adj.shape[1]), owners, axis=0),
        chips,
        on_diagonal,
    )
    outlet_share = outlet_share.T.reshape(local_heads, head_width, -1)
    attended_slope = head_order(attended_slope.reshape(length, local_heads, head_width))
    query_adj, key_adj, value_adj = lax.map(
        partial(head_backward, allowed, scale_factor),
        (queries, keys_rot, values_v, attended_slope, log_totals),
    )
    query_adj = rotate(head_order(query_adj), cosine, -sine_part)
    key_adj = rotate(head_order(key_adj), cosine, -sine_part)
    mixed_slope = (
        jnp.stack([query_adj, key_adj, head_order(value_adj)], axis=1)
        .astype(low)
        .reshape(length, -1)
    )
    inlet_adj = lax.dot_general(
        normed_all, mixed_slope, (((0,), (0,)), ((), ())), preferred_element_type=f32
    )
    inlet_share = scatter_shards(
        jnp.take(inlet_adj.reshape(trees, -1, inlet_adj.shape[1]), owners, axis=0),
        chips,
        on_diagonal,
    ).reshape(-1, 3, local_heads, head_width)
    normed_slope = shared(
        lax.dot_general(
            mixed_slope, inlet_flat, (((1,), (1,)), ((), ())), preferred_element_type=f32
        )
    )
    values_back = jax.vjp(modulate, values, norm_one, shifts[0], shifts[1])[1]
    values_adj, gain_one_adj, shift_one_adj, scale_one_adj = values_back(normed_slope)
    adjoint_tokens = diagonal((middle_slope + values_adj).astype(low))
    sums = jnp.stack(
        [
            shift_one_adj,
            scale_one_adj,
            gate_one_adj,
            shift_two_adj,
            scale_two_adj,
            gate_two_adj,
            gain_one_adj,
            gain_two_adj,
            down_bias_adj,
        ]
    )
    sums = sums.reshape(9, devices, slim).transpose(1, 0, 2).reshape(devices, 9 * slim)
    bias_rows = jnp.take(up_bias_adj.reshape(trees, units), spots, axis=0)
    bias_rows = jnp.where(
        jnp.arange(2)[None, :, None] == core, bias_rows[:, None, :], 0.0
    ).reshape(devices, units)
    back = exchange_small(jnp.concatenate([sums, bias_rows], axis=1)).reshape(
        chips, 2, 2, 9 * slim + units
    )
    dmods = jnp.sum(back[..., : 6 * slim], axis=1).reshape(trees, 6 * slim)
    rest = jnp.sum(back[..., 6 * slim :].reshape(devices, -1), axis=0)
    mod_bias_share = jnp.sum(dmods, axis=0).reshape(6, slim)
    mod_weight_share = lax.dot_general(
        embeds_act, dmods, (((0,), (0,)), ((), ())), precision=HIGHEST
    ).reshape(-1, 6, slim)
    return (
        layer_output,
        adjoint_tokens,
        rest[:slim],
        inlet_share,
        outlet_share,
        rest[slim : 2 * slim],
        up_share,
        rest[3 * slim :],
        down_share,
        rest[2 * slim : 3 * slim],
        mod_weight_share,
        mod_bias_share,
    )


def solution(mesh):
    chips = mesh.shape["dp"] // 2
    whole = Mesh(mesh.devices.reshape(chips, 2, mesh.shape["tensor"]), ALL)
    dp = ("chip", "core")
    in_specs = (
        P(ALL, None),
        P(ALL, None),
        P(dp, None),
        P(dp, None),
        P(dp),
        P(ALL),
        P(dp, None, "tensor", None),
        P("tensor", None, dp),
        P(ALL),
        P(None, ALL),
        P(ALL),
        P(ALL, None),
        P(ALL),
        P(None, None, ALL),
        P(None, ALL),
    )
    out_specs = (
        P(ALL, None),
        P(ALL, None),
        P(ALL),
        P(dp, None, "tensor", None),
        P("tensor", None, dp),
        P(ALL),
        P(None, ALL),
        P(ALL),
        P(ALL, None),
        P(ALL),
        P(None, None, ALL),
        P(None, ALL),
    )
    return jax.shard_map(
        partial(per_device, chips),
        mesh=whole,
        in_specs=in_specs,
        out_specs=out_specs,
        check_vma=False,
    )
```

time: 1270 us -> 797 us (0.63)
  waiting for transfers between devices: 596 us -> 135 us
  blocking collectives: 238 us -> 0 us
  starting transfers between devices: 2.2 us -> 105 us
  other arithmetic: 77.1 us -> 175 us
  local copies, waits for them, and re-layouts: 54 us -> 122 us
  matrix products: 285 us -> 247 us
  between operations: 16.4 us -> 2.95 us
    reduce_scatter x9 -> x0, waiting for transfers between devices: 440 us -> none  [the longest x1 105 us: per_device(): lax.psum_scatter(mod_weight_adj, ('dp', 'tensor'), scatter_dimension=2, t...]
    all_gather x8 -> x0, waiting for transfers between devices: 153 us -> none  [the longest x1 41.2 us: per_device(): normed_two_all = lax.all_gather(normed_two, 'tensor', axis=0, tiled=True)]
    unnamed x4 -> x0, blocking collectives: 148 us -> none
    ppermute x0 -> x52, waiting for transfers between devices: none -> 135 us  [the longest x24 128 us: partner(): return lax.ppermute(array, 'chip', [(i, i ^ mask) for i in range(chips)])]
    ppermute x0 -> x52, starting transfers between devices: none -> 90.6 us  [the longest x12 46 us: diagonal(): return lax.ppermute(array, CROSS, DIAGONAL)]
    all_gather x2 -> x0, blocking collectives: 90 us -> none  [the longest x1 67.6 us: per_device(): lax.all_gather(modulator_bias, ('dp', 'tensor'), axis=1, tiled=True)]
    convert_element_type x11 -> x13, other arithmetic: 11.2 us -> 71.3 us  [the longest x6 60.1 us: head_forward(): probs.astype(jnp.bfloat16)]
    dot_general x29 -> x16, matrix products: 116 us -> 81.4 us  [the longest x1 15.9 us: per_device(): lax.dot_general(mlp_slope_all, down_full, (((1,), (1,)), ((), ())), prefe...]
  transfers between devices with their start and end apart: 17 -> 55, of which waited for: 13 -> 18; matrix products, arithmetic and copies ran while one was open for 9% -> 64% of each run, Pallas kernels for 0% -> 0%
where the time goes in v1:
time: 797 us; the launch traced here: 787 us
  matrix products  247 us (31%)
  other arithmetic  175 us (22%)
  waiting for transfers between devices  135 us (17%)
  local copies, waits for them, and re-layouts  122 us (15%)
  starting transfers between devices  105 us (13%)
    ppermute x24, waiting for transfers between devices, partner(): return lax.ppermute(array, 'chip', [(i, i ^ mask) for i in range(chips)])  128 us
    convert_element_type x6, other arithmetic, head_forward(): probs.astype(jnp.bfloat16)  60.1 us
    ppermute x12, starting transfers between devices, diagonal(): return lax.ppermute(array, CROSS, DIAGONAL)  46 us
    unnamed x221, local copies, waits for them, and re-layouts  37.8 us
    dot_general x6, matrix products, head_backward(): jnp.dot(score_slope.T, queries, preferred_element_type=jnp.float32)  35.2 us
    ppermute x24, starting transfers between devices, partner(): return lax.ppermute(array, 'chip', [(i, i ^ mask) for i in range(chips)])  29.3 us
    dot_general x6, matrix products, head_forward(): jnp.dot(probs.astype(jnp.bfloat16), values_v, preferred_element_type=jnp....  29.1 us
    dot_general x6, matrix products, head_backward(): scores = jnp.dot(queries, keys_rot.T, preferred_element_type=jnp.float32)  28.6 us
  transfers between devices with their start and end apart: 55, of which 18 were waited for; matrix products, arithmetic and copies ran while one was open for 64% of the time, Pallas kernels for 0%

profile of v1, /device:TPU:0, one launch (start us, length us, event | category | flops | bytes accessed | tf_op | source)
XLA Modules:
  0.0 787.3 jit_solution(3637818038278692674)
XLA Ops:
  13.6 4.9 all-to-all-start
  28.6 5.9 all-to-all-start.1
  56.2 12.0 %collective-permute-start.26 = (bf16[896,768]{1,0:T(8,128)(2,1)}, bf16[896,768]{1,0:T(8,128)(2,1)}, u32[]{:S(2)}, u32[]{:S(2)}) collective-permute-start(bf16[896,768]{1,0:T(8,128)(2,1)} %param.24), channel_id=1, source_target_pairs={{0,0},{1,2},{2,1},{3,3},{4,4},{5,6},{6,5},{7,7},{8,8},{9,10},{10,9... | collective-permute-start | bytes 4128776 | tf_op jit(solution)/shard_map/ppermute | solution.py:88
  75.5 7.0 collective-permute-done.4
  86.7 13.5 %collective-permute-done.5 = bf16[4,48,1152]{2,1,0:T(8,128)(2,1)S(1)} collective-permute-done((bf16[4,48,1152]{2,1,0:T(8,128)(2,1)S(1)}, bf16[4,48,1152]{2,1,0:T(8,128)(2,1)S(1)}, u32[]{:S(2)}, u32[]{:S(2)}) %collective-permute-start.5) | collective-permute-done | bytes 442400 | tf_op jit(solution)/shard_map/ppermute | solution.py:105
  111.3 5.2 collective-permute-done.6
  126.7 5.3 fusion.71
  146.8 143.7 %while.28 = (s32[]{:T(128)}, bf16[6,1792,64]{1,2,0:T(8,128)(2,1)}, f32[6,1792]{1,0:T(8,128)}, bf16[6,1792,64]{2,1,0:T(8,128)(2,1)S(1)}, bf16[6,1792,64]{2,1,0:T(...) while((s32[]{:T(128)}, bf16[6,1792,64]{1,2,0:T(8,128)(2,1)}, ...), condition=%wide.region_6.7_spmd.clone, body=%wide.region_3.6_spmd.clone.sunk | while | flops 860731648 | bytes 104533120 | solution.py:244
  156.0 10.0 %divide_convert_fusion.2 = bf16[1792,1792]{0,1:T(8,128)(2,1)} fusion(f32[1792,1792]{0,1:T(8,128)} %copy-done.2, f32[1792]{0:T(1024)S(1)} %fusion.173, f32[1792]{0:T(1024)S(1)} %get-tuple-element.475, pred[1792,14]{0,1:T(8,128)(4,1)S(1)} %get-tuple-element.512), kind=kLoop, calls=%fused_computation.12.clone.1 | loop fusion | flops 16056320 | bytes 19307008 | tf_op jit(solution)/shard_map/while/body/eval_jaxpr/convert_element_type | solution.py:62
  166.1 4.8 fusion.174
  179.9 10.0 %divide_convert_fusion.2 = bf16[1792,1792]{0,1:T(8,128)(2,1)} fusion(f32[1792,1792]{0,1:T(8,128)} %copy-done.2, f32[1792]{0:T(1024)S(1)} %fusion.173, f32[1792]{0:T(1024)S(1)} %get-tuple-element.475, pred[1792,14]{0,1:T(8,128)(4,1)S(1)} %get-tuple-element.512), kind=kLoop, calls=%fused_computation.12.clone.1 | loop fusion | flops 16056320 | bytes 19307008 | tf_op jit(solution)/shard_map/while/body/eval_jaxpr/convert_element_type | solution.py:62
  189.9 4.8 fusion.174
  203.8 10.0 %divide_convert_fusion.2 = bf16[1792,1792]{0,1:T(8,128)(2,1)} fusion(f32[1792,1792]{0,1:T(8,128)} %copy-done.2, f32[1792]{0:T(1024)S(1)} %fusion.173, f32[1792]{0:T(1024)S(1)} %get-tuple-element.475, pred[1792,14]{0,1:T(8,128)(4,1)S(1)} %get-tuple-element.512), kind=kLoop, calls=%fused_computation.12.clone.1 | loop fusion | flops 16056320 | bytes 19307008 | tf_op jit(solution)/shard_map/while/body/eval_jaxpr/convert_element_type | solution.py:62
  213.8 4.8 fusion.174
  227.6 10.0 %divide_convert_fusion.2 = bf16[1792,1792]{0,1:T(8,128)(2,1)} fusion(f32[1792,1792]{0,1:T(8,128)} %copy-done.2, f32[1792]{0:T(1024)S(1)} %fusion.173, f32[1792]{0:T(1024)S(1)} %get-tuple-element.475, pred[1792,14]{0,1:T(8,128)(4,1)S(1)} %get-tuple-element.512), kind=kLoop, calls=%fused_computation.12.clone.1 | loop fusion | flops 16056320 | bytes 19307008 | tf_op jit(solution)/shard_map/while/body/eval_jaxpr/convert_element_type | solution.py:62
  237.6 4.8 fusion.174
  251.5 10.0 %divide_convert_fusion.2 = bf16[1792,1792]{0,1:T(8,128)(2,1)} fusion(f32[1792,1792]{0,1:T(8,128)} %copy-done.2, f32[1792]{0:T(1024)S(1)} %fusion.173, f32[1792]{0:T(1024)S(1)} %get-tuple-element.475, pred[1792,14]{0,1:T(8,128)(4,1)S(1)} %get-tuple-element.512), kind=kLoop, calls=%fused_computation.12.clone.1 | loop fusion | flops 16056320 | bytes 19307008 | tf_op jit(solution)/shard_map/while/body/eval_jaxpr/convert_element_type | solution.py:62
  261.5 4.8 fusion.174
  275.3 10.0 %divide_convert_fusion.2 = bf16[1792,1792]{0,1:T(8,128)(2,1)} fusion(f32[1792,1792]{0,1:T(8,128)} %copy-done.2, f32[1792]{0:T(1024)S(1)} %fusion.173, f32[1792]{0:T(1024)S(1)} %get-tuple-element.475, pred[1792,14]{0,1:T(8,128)(4,1)S(1)} %get-tuple-element.512), kind=kLoop, calls=%fused_computation.12.clone.1 | loop fusion | flops 16056320 | bytes 19307008 | tf_op jit(solution)/shard_map/while/body/eval_jaxpr/convert_element_type | solution.py:62
  285.4 4.8 fusion.174
  303.2 12.0 %collective-permute-done.17 = bf16[4,96,768]{2,1,0:T(8,128)(2,1)S(1)} collective-permute-done((bf16[4,96,768]{2,1,0:T(8,128)(2,1)S(1)}, bf16[4,96,768]{2,1,0:T(8,128)(2,1)S(1)}, u32[]{:S(2)}, u32[]{:S(2)}) %collective-permute-start.17) | collective-permute-done | bytes 589856 | tf_op jit(solution)/shard_map/ppermute | solution.py:105
  317.9 6.7 collective-permute-done.22
  334.4 10.9 %collective-permute-done.18 = bf16[8,96,768]{2,1,0:T(8,128)(2,1)S(1)} collective-permute-done((bf16[8,96,768]{2,1,0:T(8,128)(2,1)S(1)}, bf16[8,96,768]{2,1,0:T(8,128)(2,1)S(1)}, u32[]{:S(2)}, u32[]{:S(2)}) %collective-permute-start.18) | collective-permute-done | bytes 1179680 | tf_op jit(solution)/shard_map/ppermute | solution.py:105
  345.3 17.7 %collective-permute-done.23 = bf16[8,96,768]{2,1,0:T(8,128)(2,1)S(1)} collective-permute-done((bf16[8,96,768]{2,1,0:T(8,128)(2,1)S(1)}, bf16[8,96,768]{2,1,0:T(8,128)(2,1)S(1)}, u32[]{:S(2)}, u32[]{:S(2)}) %collective-permute-start.23) | collective-permute-done | bytes 1179680 | tf_op jit(solution)/shard_map/ppermute | solution.py:105
  372.2 11.4 %multiply_convert_fusion.1 = (bf16[1792,1536]{1,0:T(8,128)(2,1)S(1)}, f32[1792,1536]{1,0:T(8,128)}) fusion(f32[1536]{0:T(1024)S(1)} %add.425, bf16[1536,768]{1,0:T(8,128)(2,1)} %bitcast.363, bf16[896,768]{1,0:T(8,128)(2,1)} %collective-permute-done.13, bf16[896,768]{1,0:T(8,128)(2,1)} %add_convert_fusion.2), kind=kOutput, calls=%fused_computation.72 | convolution fusion | flops 4260888576 | bytes 21633024 | tf_op jit(solution)/shard_map/dot_general | solution.py:257
  383.6 6.6 fusion.74
  392.9 15.9 %convert_reduce_fusion = (f32[1536]{0:T(1024)S(1)}, bf16[1792,1536]{1,0:T(8,128)(2,1)}) fusion(f32[1792,1536]{1,0:T(8,128)} %get-tuple-element.371, f32[1536]{0:T(1024)S(1)} %add.425, bf16[1536,768]{1,0:T(8,128)(2,1)S(1)} %bitcast.361, bf16[896,768]{1,0:T(8,128)(2,1)} %collective-permute-done.27, bf16[896,768]{1,0:T(8,128)(2,1)} %fusion.68), kind=kOutput, calls=%fused_computation.71 | convolution fusion | flops 4296669696 | bytes 21639168 | tf_op jit(solution)/shard_map/dot_general | solution.py:269
  408.8 7.2 fusion.126
  416.0 8.5 %fusion.75 = f32[1536,768]{1,0:T(8,128)S(1)} fusion(bf16[1792,1536]{1,0:T(8,128)(2,1)S(1)} %copy-done.87, bf16[896,768]{1,0:T(8,128)(2,1)} %collective-permute-done.13, bf16[896,768]{1,0:T(8,128)(2,1)} %add_convert_fusion.2), kind=kOutput, calls=%fused_computation.133 | convolution fusion | flops 4233363456 | bytes 12976128 | tf_op jit(solution)/shard_map/dot_general | solution.py:280
  441.6 4.8 collective-permute-done.42
  457.9 5.4 convert_reduce_fusion.1
  467.9 11.8 %collective-permute-start.25 = (bf16[896,768]{1,0:T(8,128)(2,1)}, bf16[896,768]{1,0:T(8,128)(2,1)}, u32[]{:S(2)}, u32[]{:S(2)}) collective-permute-start(bf16[896,768]{1,0:T(8,128)(2,1)} %get-tuple-element.329), channel_id=1, source_target_pairs={{0,0},{1,2},{2,1},{3,3},{4,4},{5,6},{6,5},{7,7},{8,8},{9,10},{10,9... | collective-permute-start | bytes 4128776 | tf_op jit(solution)/shard_map/ppermute | solution.py:88
  485.6 18.4 %collective-permute-done.49 = bf16[2,96,768]{2,1,0:T(8,128)(2,1)S(1)} collective-permute-done((bf16[2,96,768]{2,1,0:T(8,128)(2,1)S(1)}, bf16[2,96,768]{2,1,0:T(8,128)(2,1)S(1)}, u32[]{:S(2)}, u32[]{:S(2)}) %collective-permute-start.49) | collective-permute-done | bytes 294944 | tf_op jit(solution)/shard_map/ppermute | solution.py:105
  532.3 147.7 %while.29 = (s32[]{:T(128)}, f32[6,1792,64]{1,2,0:T(8,128)}, f32[6,1792,64]{1,2,0:T(8,128)}, bf16[6,1792,64]{1,2,0:T(8,128)(2,1)S(1)}, bf16[6,1792,64]{2,1,0:T(8...) while((s32[]{:T(128)}, f32[6,1792,64]{1,2,0:T(8,128)}, ...), condition=%wide.region_13.15_spmd.clone, body=%wide.region_11.14_spmd.clone.sunk | while | flops 2087319808 | bytes 126681736 | solution.py:303
  544.9 5.9 fusion.185
  569.5 5.9 fusion.185
  585.4 4.8 multiply_reduce_fusion.7
  594.1 5.9 fusion.185
  618.7 5.9 fusion.185
  634.7 4.8 multiply_reduce_fusion.7
  643.4 5.9 fusion.185
  668.0 5.9 fusion.185
  686.4 5.5 fusion.128
  691.9 4.8 gather_fusion.6
  709.9 12.4 %collective-permute-done.32 = bf16[8,48,1152]{2,1,0:T(8,128)(2,1)S(1)} collective-permute-done((bf16[8,48,1152]{2,1,0:T(8,128)(2,1)S(1)}, bf16[8,48,1152]{2,1,0:T(8,128)(2,1)S(1)}, u32[]{:S(2)}, u32[]{:S(2)}) %collective-permute-start.32) | collective-permute-done | bytes 884768 | tf_op jit(solution)/shard_map/ppermute | solution.py:105
  730.3 8.3 %collective-permute-done.33 = bf16[4,48,1152]{2,1,0:T(8,128)(2,1)} collective-permute-done((bf16[4,48,1152]{2,1,0:T(8,128)(2,1)}, bf16[4,48,1152]{2,1,0:T(8,128)(2,1)}, u32[]{:S(2)}, u32[]{:S(2)}) %collective-permute-start.33) | collective-permute-done | bytes 442400 | tf_op jit(solution)/shard_map/ppermute | solution.py:105
  758.4 11.8 %collective-permute-start.31 = (bf16[896,768]{1,0:T(8,128)(2,1)}, bf16[896,768]{1,0:T(8,128)(2,1)}, u32[]{:S(2)}, u32[]{:S(2)}) collective-permute-start(bf16[896,768]{1,0:T(8,128)(2,1)} %add_convert_fusion), channel_id=1, source_target_pairs={{0,0},{1,2},{2,1},{3,3},{4,4},{5,6},{6,5},{7,7},{8,8},{9,10},{10,9... | collective-permute-start | bytes 4128776 | tf_op jit(solution)/shard_map/ppermute | solution.py:88
  774.2 6.8 collective-permute-done.36
  (629 shorter events, 408.8 us)
Async XLA Ops:
  2.0 39.5 %collective-permute-start.2 = (bf16[48,1152]{1,0:T(8,128)(2,1)S(1)}, bf16[48,1152]{1,0:T(8,128)(2,1)S(1)}, u32[]{:S(2)}, u32[]{:S(2)}) collective-permute-start(bf16[48,1152]{1,0:T(8,128)(2,1)S(1)} %reshape.600), channel_id=1, source_target_pairs={{0,0},{1,2},{2,1},{3,3},{4,4},{5,6},{6,5},{7,7},{8,8},{9,10},{10,9... | collective-permute-start | bytes 331784 | tf_op jit(solution)/shard_map/ppermute | solution.py:88
  2.7 41.1 %collective-permute-start.3 = (bf16[48,1152]{1,0:T(8,128)(2,1)S(1)}, bf16[48,1152]{1,0:T(8,128)(2,1)S(1)}, u32[]{:S(2)}, u32[]{:S(2)}) collective-permute-start(bf16[48,1152]{1,0:T(8,128)(2,1)S(1)} %reshape.600), channel_id=1, source_target_pairs={{0,1},{2,0},{3,2},{1,3},{4,5},{6,4},{7,6},{5,7},{8,9},{10,8},{11,1... | collective-permute-start | bytes 331784 | tf_op jit(solution)/shard_map/ppermute | solution.py:109
  7.9 29.8 %collective-permute-start.7 = (bf16[48,384]{1,0:T(8,128)(2,1)S(1)}, bf16[48,384]{1,0:T(8,128)(2,1)S(1)}, u32[]{:S(2)}, u32[]{:S(2)}) collective-permute-start(bf16[48,384]{1,0:T(8,128)(2,1)S(1)} %bitcast.358), channel_id=1, source_target_pairs={{0,0},{1,2},{2,1},{3,3},{4,4},{5,6},{6,5},{7,7},{8,8},{9,10},{10,9... | collective-permute-start | bytes 110600 | tf_op jit(solution)/shard_map/ppermute | solution.py:88
  8.6 31.6 %collective-permute-start.8 = (bf16[48,384]{1,0:T(8,128)(2,1)S(1)}, bf16[48,384]{1,0:T(8,128)(2,1)S(1)}, u32[]{:S(2)}, u32[]{:S(2)}) collective-permute-start(bf16[48,384]{1,0:T(8,128)(2,1)S(1)} %bitcast.359), channel_id=1, source_target_pairs={{0,1},{2,0},{3,2},{1,3},{4,5},{6,4},{7,6},{5,7},{8,9},{10,8},{11,1... | collective-permute-start | bytes 110600 | tf_op jit(solution)/shard_map/ppermute | solution.py:109
  13.6 12.3 %all-to-all-start = ((f32[32,1,142]{2,1,0:T(1,128)}), f32[32,1,142]{2,1,0:T(1,128)S(1)}, u32[]{:S(2)}, u32[]{:S(2)}) async-start(f32[32,1,142]{2,1,0:T(1,128)} %broadcast_in_dim.210), calls=%async_computation | async-start | bytes 65536 | tf_op jit(solution)/shard_map/all_to_all | solution.py:135
  18.5 37.7 %collective-permute-start.14 = (bf16[96,768]{1,0:T(8,128)(2,1)}, bf16[96,768]{1,0:T(8,128)(2,1)S(1)}, u32[]{:S(2)}, u32[]{:S(2)}) collective-permute-start(bf16[96,768]{1,0:T(8,128)(2,1)} %bitcast.366), channel_id=1, source_target_pairs={{0,0},{1,2},{2,1},{3,3},{4,4},{5,6},{6,5},{7,7},{8,8},{9,10},{10,9... | collective-permute-start | bytes 442376 | tf_op jit(solution)/shard_map/ppermute | solution.py:88
  28.6 24.4 %all-to-all-start.1 = ((f32[32,1,312]{2,1,0:T(1,128)}), f32[32,1,312]{2,1,0:T(1,128)S(1)}, u32[]{:S(2)}, u32[]{:S(2)}) async-start(f32[32,1,312]{2,1,0:T(1,128)} %all_to_all.19), calls=%async_computation.1 | async-start | bytes 98304 | tf_op jit(solution)/shard_map/all_to_all | solution.py:135
  37.8 33.1 %collective-permute-start.15 = (bf16[96,768]{1,0:T(8,128)(2,1)S(1)}, bf16[96,768]{1,0:T(8,128)(2,1)S(1)}, u32[]{:S(2)}, u32[]{:S(2)}) collective-permute-start(bf16[96,768]{1,0:T(8,128)(2,1)S(1)} %bitcast.367), channel_id=1, source_target_pairs={{0,1},{2,0},{3,2},{1,3},{4,5},{6,4},{7,6},{5,7},{8,9},{10,8},{11,1... | collective-permute-start | bytes 442376 | tf_op jit(solution)/shard_map/ppermute | solution.py:109
  40.2 28.7 %collective-permute-start.19 = (bf16[96,768]{1,0:T(8,128)(2,1)S(1)}, bf16[96,768]{1,0:T(8,128)(2,1)S(1)}, u32[]{:S(2)}, u32[]{:S(2)}) collective-permute-start(bf16[96,768]{1,0:T(8,128)(2,1)S(1)} %copy-done.86), channel_id=1, source_target_pairs={{0,0},{1,2},{2,1},{3,3},{4,4},{5,6},{6,5},{7,7},{8,8},{9,10},{10,9... | collective-permute-start | bytes 442376 | tf_op jit(solution)/shard_map/ppermute | solution.py:88
  41.5 32.5 %collective-permute-start.20 = (bf16[96,768]{1,0:T(8,128)(2,1)S(1)}, bf16[96,768]{1,0:T(8,128)(2,1)S(1)}, u32[]{:S(2)}, u32[]{:S(2)}) collective-permute-start(bf16[96,768]{1,0:T(8,128)(2,1)S(1)} %copy-done.86), channel_id=1, source_target_pairs={{0,1},{2,0},{3,2},{1,3},{4,5},{6,4},{7,6},{5,7},{8,9},{10,8},{11,1... | collective-permute-start | bytes 442376 | tf_op jit(solution)/shard_map/ppermute | solution.py:109
  50.4 52.2 %collective-permute-start = (bf16[896,768]{1,0:T(8,128)(2,1)}, bf16[896,768]{1,0:T(8,128)(2,1)S(1)}, u32[]{:S(2)}, u32[]{:S(2)}) collective-permute-start(bf16[896,768]{1,0:T(8,128)(2,1)} %param.23), channel_id=1, source_target_pairs={{0,0},{1,2},{2,1},{3,3},{4,4},{5,6},{6,5},{7,7},{8,8},{9,10},{10,9... | collective-permute-start | bytes 4128776 | tf_op jit(solution)/shard_map/ppermute | solution.py:88
  56.2 273.4 %collective-permute-start.26 = (bf16[896,768]{1,0:T(8,128)(2,1)}, bf16[896,768]{1,0:T(8,128)(2,1)}, u32[]{:S(2)}, u32[]{:S(2)}) collective-permute-start(bf16[896,768]{1,0:T(8,128)(2,1)} %param.24), channel_id=1, source_target_pairs={{0,0},{1,2},{2,1},{3,3},{4,4},{5,6},{6,5},{7,7},{8,8},{9,10},{10,9... | collective-permute-start | bytes 4128776 | tf_op jit(solution)/shard_map/ppermute | solution.py:88
  68.8 13.6 %collective-permute-start.4 = (bf16[2,48,1152]{2,1,0:T(8,128)(2,1)S(1)}, bf16[2,48,1152]{2,1,0:T(8,128)(2,1)S(1)}, u32[]{:S(2)}, u32[]{:S(2)}) collective-permute-start(bf16[2,48,1152]{2,1,0:T(8,128)(2,1)S(1)} %pad_maximum_fusion.20), channel_id=1, source_target_pairs={{0,16},{4,20},{8,24},{12,28},{16,0},{20,4},{24,8},{28,12},{1,17},{... | collective-permute-start | bytes 663560 | tf_op jit(solution)/shard_map/ppermute | solution.py:105
  70.9 11.7 %collective-permute-start.10 = (bf16[4,48,384]{2,1,0:T(8,128)(2,1)S(1)}, bf16[4,48,384]{2,1,0:T(8,128)(2,1)S(1)}, u32[]{:S(2)}, u32[]{:S(2)}) collective-permute-start(bf16[4,48,384]{2,1,0:T(8,128)(2,1)S(1)} %pad_maximum_fusion.21), channel_id=1, source_target_pairs={{0,8},{4,12},{8,0},{12,4},{16,24},{20,28},{24,16},{28,20},{1,9},{5... | collective-permute-start | bytes 442376 | tf_op jit(solution)/shard_map/ppermute | solution.py:105
  74.0 221.9 %collective-permute-start.16 = (bf16[2,96,768]{2,1,0:T(8,128)(2,1)}, bf16[2,96,768]{2,1,0:T(8,128)(2,1)}, u32[]{:S(2)}, u32[]{:S(2)}) collective-permute-start(bf16[2,96,768]{2,1,0:T(8,128)(2,1)} %pad_maximum_fusion.18), channel_id=1, source_target_pairs={{0,16},{4,20},{8,24},{12,28},{16,0},{20,4},{24,8},{28,12},{1,17},{... | collective-permute-start | bytes 884744 | tf_op jit(solution)/shard_map/ppermute | solution.py:105
  82.5 216.5 %collective-permute-start.21 = (bf16[2,96,768]{2,1,0:T(8,128)(2,1)}, bf16[2,96,768]{2,1,0:T(8,128)(2,1)S(1)}, u32[]{:S(2)}, u32[]{:S(2)}) collective-permute-start(bf16[2,96,768]{2,1,0:T(8,128)(2,1)} %pad_maximum_fusion.19), channel_id=1, source_target_pairs={{0,16},{4,20},{8,24},{12,28},{16,0},{20,4},{24,8},{28,12},{1,17},{... | collective-permute-start | bytes 884744 | tf_op jit(solution)/shard_map/ppermute | solution.py:105
  82.6 17.6 %collective-permute-start.5 = (bf16[4,48,1152]{2,1,0:T(8,128)(2,1)S(1)}, bf16[4,48,1152]{2,1,0:T(8,128)(2,1)S(1)}, u32[]{:S(2)}, u32[]{:S(2)}) collective-permute-start(bf16[4,48,1152]{2,1,0:T(8,128)(2,1)S(1)} %pad_maximum_fusion.16), channel_id=1, source_target_pairs={{0,8},{4,12},{8,0},{12,4},{16,24},{20,28},{24,16},{28,20},{1,9},{5... | collective-permute-start | bytes 1327112 | tf_op jit(solution)/shard_map/ppermute | solution.py:105
  102.7 13.8 %collective-permute-start.6 = (bf16[8,48,1152]{2,1,0:T(8,128)(2,1)}, bf16[8,48,1152]{2,1,0:T(8,128)(2,1)}, u32[]{:S(2)}, u32[]{:S(2)}) collective-permute-start(bf16[8,48,1152]{2,1,0:T(8,128)(2,1)} %pad_maximum_fusion.13), channel_id=1, source_target_pairs={{0,4},{4,0},{8,12},{12,8},{16,20},{20,16},{24,28},{28,24},{1,5},{5... | collective-permute-start | bytes 2654216 | tf_op jit(solution)/shard_map/ppermute | solution.py:105
  106.9 19.8 %collective-permute-start.1 = (bf16[896,768]{1,0:T(8,128)(2,1)S(1)}, bf16[896,768]{1,0:T(8,128)(2,1)}, u32[]{:S(2)}, u32[]{:S(2)}) collective-permute-start(bf16[896,768]{1,0:T(8,128)(2,1)S(1)} %fusion.63), channel_id=1, source_target_pairs={{0,2},{2,0},{1,3},{3,1},{4,6},{6,4},{5,7},{7,5},{8,10},{10,8},{9,1... | collective-permute-start | bytes 4128776 | tf_op jit(solution)/shard_map/ppermute | solution.py:92
  295.0 31.3 %collective-permute-start.12 = (bf16[896,768]{1,0:T(8,128)(2,1)S(1)}, bf16[896,768]{1,0:T(8,128)(2,1)S(1)}, u32[]{:S(2)}, u32[]{:S(2)}) collective-permute-start(bf16[896,768]{1,0:T(8,128)(2,1)S(1)} %slice.530), channel_id=1, source_target_pairs={{0,2},{2,0},{1,3},{3,1},{4,6},{6,4},{5,7},{7,5},{8,10},{10,8},{9,1... | collective-permute-start | bytes 4128776 | tf_op jit(solution)/shard_map/ppermute | solution.py:92
  298.9 16.3 %collective-permute-start.17 = (bf16[4,96,768]{2,1,0:T(8,128)(2,1)S(1)}, bf16[4,96,768]{2,1,0:T(8,128)(2,1)S(1)}, u32[]{:S(2)}, u32[]{:S(2)}) collective-permute-start(bf16[4,96,768]{2,1,0:T(8,128)(2,1)S(1)} %pad_maximum_fusion.14), channel_id=1, source_target_pairs={{0,8},{4,12},{8,0},{12,4},{16,24},{20,28},{24,16},{28,20},{1,9},{5... | collective-permute-start | bytes 1769480 | tf_op jit(solution)/shard_map/ppermute | solution.py:105
  299.1 25.4 %collective-permute-start.22 = (bf16[4,96,768]{2,1,0:T(8,128)(2,1)S(1)}, bf16[4,96,768]{2,1,0:T(8,128)(2,1)S(1)}, u32[]{:S(2)}, u32[]{:S(2)}) collective-permute-start(bf16[4,96,768]{2,1,0:T(8,128)(2,1)S(1)} %pad_maximum_fusion.15), channel_id=1, source_target_pairs={{0,8},{4,12},{8,0},{12,4},{16,24},{20,28},{24,16},{28,20},{1,9},{5... | collective-permute-start | bytes 1769480 | tf_op jit(solution)/shard_map/ppermute | solution.py:105
  316.3 28.9 %collective-permute-start.18 = (bf16[8,96,768]{2,1,0:T(8,128)(2,1)S(1)}, bf16[8,96,768]{2,1,0:T(8,128)(2,1)S(1)}, u32[]{:S(2)}, u32[]{:S(2)}) collective-permute-start(bf16[8,96,768]{2,1,0:T(8,128)(2,1)S(1)} %pad_maximum_fusion.11), channel_id=1, source_target_pairs={{0,4},{4,0},{8,12},{12,8},{16,20},{20,16},{24,28},{28,24},{1,5},{5... | collective-permute-start | bytes 3538952 | tf_op jit(solution)/shard_map/ppermute | solution.py:105
  324.7 38.4 %collective-permute-start.23 = (bf16[8,96,768]{2,1,0:T(8,128)(2,1)S(1)}, bf16[8,96,768]{2,1,0:T(8,128)(2,1)S(1)}, u32[]{:S(2)}, u32[]{:S(2)}) collective-permute-start(bf16[8,96,768]{2,1,0:T(8,128)(2,1)S(1)} %pad_maximum_fusion.12), channel_id=1, source_target_pairs={{0,4},{4,0},{8,12},{12,8},{16,20},{20,16},{24,28},{28,24},{1,5},{5... | collective-permute-start | bytes 3538952 | tf_op jit(solution)/shard_map/ppermute | solution.py:105
  329.6 42.6 %collective-permute-start.13 = (bf16[896,768]{1,0:T(8,128)(2,1)}, bf16[896,768]{1,0:T(8,128)(2,1)}, u32[]{:S(2)}, u32[]{:S(2)}) collective-permute-start(bf16[896,768]{1,0:T(8,128)(2,1)} %add_convert_fusion.2), channel_id=1, source_target_pairs={{0,2},{2,0},{1,3},{3,1},{4,6},{6,4},{5,7},{7,5},{8,10},{10,8},{9,1... | collective-permute-start | bytes 4128776 | tf_op jit(solution)/shard_map/ppermute | solution.py:92
  332.3 51.3 %collective-permute-start.27 = (bf16[896,768]{1,0:T(8,128)(2,1)}, bf16[896,768]{1,0:T(8,128)(2,1)}, u32[]{:S(2)}, u32[]{:S(2)}) collective-permute-start(bf16[896,768]{1,0:T(8,128)(2,1)} %fusion.68), channel_id=1, source_target_pairs={{0,2},{2,0},{1,3},{3,1},{4,6},{6,4},{5,7},{7,5},{8,10},{10,8},{9,1... | collective-permute-start | bytes 4128776 | tf_op jit(solution)/shard_map/ppermute | solution.py:92
  391.4 47.1 %collective-permute-start.47 = (bf16[8,96,768]{2,1,0:T(8,128)(2,1)}, bf16[8,96,768]{2,1,0:T(8,128)(2,1)}, u32[]{:S(2)}, u32[]{:S(2)}) collective-permute-start(bf16[8,96,768]{2,1,0:T(8,128)(2,1)} %bitcast.77), channel_id=1, source_target_pairs={{0,4},{4,0},{8,12},{12,8},{16,20},{20,16},{24,28},{28,24},{1,5},{5... | collective-permute-start | bytes 3538952 | tf_op jit(solution)/shard_map/ppermute | solution.py:105
  425.8 20.6 %collective-permute-start.42 = (bf16[8,96,768]{2,1,0:T(8,128)(2,1)}, bf16[8,96,768]{2,1,0:T(8,128)(2,1)}, u32[]{:S(2)}, u32[]{:S(2)}) collective-permute-start(bf16[8,96,768]{2,1,0:T(8,128)(2,1)} %bitcast.72), channel_id=1, source_target_pairs={{0,4},{4,0},{8,12},{12,8},{16,20},{20,16},{24,28},{28,24},{1,5},{5... | collective-permute-start | bytes 3538952 | tf_op jit(solution)/shard_map/ppermute | solution.py:105
  427.6 22.5 %collective-permute-start.28 = (bf16[896,768]{1,0:T(8,128)(2,1)}, bf16[896,768]{1,0:T(8,128)(2,1)}, u32[]{:S(2)}, u32[]{:S(2)}) collective-permute-start(bf16[896,768]{1,0:T(8,128)(2,1)} %slice.528), channel_id=1, source_target_pairs={{0,2},{2,0},{1,3},{3,1},{4,6},{6,4},{5,7},{7,5},{8,10},{10,8},{9,1... | collective-permute-start | bytes 4128776 | tf_op jit(solution)/shard_map/ppermute | solution.py:92
  436.5 21.3 %collective-permute-start.24 = (bf16[896,768]{1,0:T(8,128)(2,1)}, bf16[896,768]{1,0:T(8,128)(2,1)}, u32[]{:S(2)}, u32[]{:S(2)}) collective-permute-start(bf16[896,768]{1,0:T(8,128)(2,1)} %slice.529), channel_id=1, source_target_pairs={{0,2},{2,0},{1,3},{3,1},{4,6},{6,4},{5,7},{7,5},{8,10},{10,8},{9,1... | collective-permute-start | bytes 4128776 | tf_op jit(solution)/shard_map/ppermute | solution.py:92
  441.0 38.7 %collective-permute-start.48 = (bf16[4,96,768]{2,1,0:T(8,128)(2,1)S(1)}, bf16[4,96,768]{2,1,0:T(8,128)(2,1)}, u32[]{:S(2)}, u32[]{:S(2)}) collective-permute-start(bf16[4,96,768]{2,1,0:T(8,128)(2,1)S(1)} %slice.534), channel_id=1, source_target_pairs={{0,8},{4,12},{8,0},{12,4},{16,24},{20,28},{24,16},{28,20},{1,9},{5... | collective-permute-start | bytes 1769480 | tf_op jit(solution)/shard_map/ppermute | solution.py:105
  449.0 33.1 %collective-permute-start.43 = (bf16[4,96,768]{2,1,0:T(8,128)(2,1)}, bf16[4,96,768]{2,1,0:T(8,128)(2,1)}, u32[]{:S(2)}, u32[]{:S(2)}) collective-permute-start(bf16[4,96,768]{2,1,0:T(8,128)(2,1)} %slice.535), channel_id=1, source_target_pairs={{0,8},{4,12},{8,0},{12,4},{16,24},{20,28},{24,16},{28,20},{1,9},{5... | collective-permute-start | bytes 1769480 | tf_op jit(solution)/shard_map/ppermute | solution.py:105
  463.3 51.4 %collective-permute-start.29 = (bf16[896,768]{1,0:T(8,128)(2,1)}, bf16[896,768]{1,0:T(8,128)(2,1)}, u32[]{:S(2)}, u32[]{:S(2)}) collective-permute-start(bf16[896,768]{1,0:T(8,128)(2,1)} %get-tuple-element.330), channel_id=1, source_target_pairs={{0,2},{2,0},{1,3},{3,1},{4,6},{6,4},{5,7},{7,5},{8,10},{10,8},{9,1... | collective-permute-start | bytes 4128776 | tf_op jit(solution)/shard_map/ppermute | solution.py:92
  467.9 261.6 %collective-permute-start.25 = (bf16[896,768]{1,0:T(8,128)(2,1)}, bf16[896,768]{1,0:T(8,128)(2,1)}, u32[]{:S(2)}, u32[]{:S(2)}) collective-permute-start(bf16[896,768]{1,0:T(8,128)(2,1)} %get-tuple-element.329), channel_id=1, source_target_pairs={{0,0},{1,2},{2,1},{3,3},{4,4},{5,6},{6,5},{7,7},{8,8},{9,10},{10,9... | collective-permute-start | bytes 4128776 | tf_op jit(solution)/shard_map/ppermute | solution.py:88
  481.3 22.7 %collective-permute-start.49 = (bf16[2,96,768]{2,1,0:T(8,128)(2,1)S(1)}, bf16[2,96,768]{2,1,0:T(8,128)(2,1)S(1)}, u32[]{:S(2)}, u32[]{:S(2)}) collective-permute-start(bf16[2,96,768]{2,1,0:T(8,128)(2,1)S(1)} %slice.537), channel_id=1, source_target_pairs={{0,16},{4,20},{8,24},{12,28},{16,0},{20,4},{24,8},{28,12},{1,17},{... | collective-permute-start | bytes 884744 | tf_op jit(solution)/shard_map/ppermute | solution.py:105
  483.4 26.9 %collective-permute-start.44 = (bf16[2,96,768]{2,1,0:T(8,128)(2,1)S(1)}, bf16[2,96,768]{2,1,0:T(8,128)(2,1)S(1)}, u32[]{:S(2)}, u32[]{:S(2)}) collective-permute-start(bf16[2,96,768]{2,1,0:T(8,128)(2,1)S(1)} %slice.538), channel_id=1, source_target_pairs={{0,16},{4,20},{8,24},{12,28},{16,0},{20,4},{24,8},{28,12},{1,17},{... | collective-permute-start | bytes 884744 | tf_op jit(solution)/shard_map/ppermute | solution.py:105
  504.1 9.9 %collective-permute-start.50 = (bf16[96,768]{1,0:T(8,128)(2,1)S(1)}, bf16[96,768]{1,0:T(8,128)(2,1)S(1)}, u32[]{:S(2)}, u32[]{:S(2)}) collective-permute-start(bf16[96,768]{1,0:T(8,128)(2,1)S(1)} %get-tuple-element.339), channel_id=1, source_target_pairs={{0,0},{1,2},{2,1},{3,3},{4,4},{5,6},{6,5},{7,7},{8,8},{9,10},{10,9... | collective-permute-start | bytes 442376 | tf_op jit(solution)/shard_map/ppermute | solution.py:88
  504.8 9.2 %collective-permute-start.51 = (bf16[96,768]{1,0:T(8,128)(2,1)S(1)}, bf16[96,768]{1,0:T(8,128)(2,1)S(1)}, u32[]{:S(2)}, u32[]{:S(2)}) collective-permute-start(bf16[96,768]{1,0:T(8,128)(2,1)S(1)} %get-tuple-element.340), channel_id=1, source_target_pairs={{1,0},{0,2},{2,3},{3,1},{5,4},{4,6},{6,7},{7,5},{9,8},{8,10},{10,1... | collective-permute-start | bytes 442376 | tf_op jit(solution)/shard_map/ppermute | solution.py:123
  511.1 212.8 %collective-permute-start.45 = (bf16[96,768]{1,0:T(8,128)(2,1)}, bf16[96,768]{1,0:T(8,128)(2,1)}, u32[]{:S(2)}, u32[]{:S(2)}) collective-permute-start(bf16[96,768]{1,0:T(8,128)(2,1)} %get-tuple-element.341), channel_id=1, source_target_pairs={{0,0},{1,2},{2,1},{3,3},{4,4},{5,6},{6,5},{7,7},{8,8},{9,10},{10,9... | collective-permute-start | bytes 442376 | tf_op jit(solution)/shard_map/ppermute | solution.py:88
  513.9 212.2 %collective-permute-start.46 = (bf16[96,768]{1,0:T(8,128)(2,1)}, bf16[96,768]{1,0:T(8,128)(2,1)}, u32[]{:S(2)}, u32[]{:S(2)}) collective-permute-start(bf16[96,768]{1,0:T(8,128)(2,1)} %get-tuple-element.342), channel_id=1, source_target_pairs={{1,0},{0,2},{2,3},{3,1},{5,4},{4,6},{6,7},{7,5},{9,8},{8,10},{10,1... | collective-permute-start | bytes 442376 | tf_op jit(solution)/shard_map/ppermute | solution.py:123
  526.2 170.6 %collective-permute-start.37 = (bf16[8,48,384]{2,1,0:T(8,128)(2,1)}, bf16[8,48,384]{2,1,0:T(8,128)(2,1)}, u32[]{:S(2)}, u32[]{:S(2)}) collective-permute-start(bf16[8,48,384]{2,1,0:T(8,128)(2,1)} %slice.539), channel_id=1, source_target_pairs={{0,4},{4,0},{8,12},{12,8},{16,20},{20,16},{24,28},{28,24},{1,5},{5... | collective-permute-start | bytes 884744 | tf_op jit(solution)/shard_map/ppermute | solution.py:105
  700.5 21.7 %collective-permute-start.32 = (bf16[8,48,1152]{2,1,0:T(8,128)(2,1)S(1)}, bf16[8,48,1152]{2,1,0:T(8,128)(2,1)S(1)}, u32[]{:S(2)}, u32[]{:S(2)}) collective-permute-start(bf16[8,48,1152]{2,1,0:T(8,128)(2,1)S(1)} %slice.533), channel_id=1, source_target_pairs={{0,4},{4,0},{8,12},{12,8},{16,20},{20,16},{24,28},{28,24},{1,5},{5... | collective-permute-start | bytes 2654216 | tf_op jit(solution)/shard_map/ppermute | solution.py:105
  709.8 31.7 %collective-permute-start.30 = (bf16[896,768]{1,0:T(8,128)(2,1)}, bf16[896,768]{1,0:T(8,128)(2,1)}, u32[]{:S(2)}, u32[]{:S(2)}) collective-permute-start(bf16[896,768]{1,0:T(8,128)(2,1)} %slice.527), channel_id=1, source_target_pairs={{0,2},{2,0},{1,3},{3,1},{4,6},{6,4},{5,7},{7,5},{8,10},{10,8},{9,1... | collective-permute-start | bytes 4128776 | tf_op jit(solution)/shard_map/ppermute | solution.py:92
  726.2 12.5 %collective-permute-start.33 = (bf16[4,48,1152]{2,1,0:T(8,128)(2,1)}, bf16[4,48,1152]{2,1,0:T(8,128)(2,1)}, u32[]{:S(2)}, u32[]{:S(2)}) collective-permute-start(bf16[4,48,1152]{2,1,0:T(8,128)(2,1)} %slice.536), channel_id=1, source_target_pairs={{0,8},{4,12},{8,0},{12,4},{16,24},{20,28},{24,16},{28,20},{1,9},{5... | collective-permute-start | bytes 1327112 | tf_op jit(solution)/shard_map/ppermute | solution.py:105
  739.8 31.8 %collective-permute-start.34 = (bf16[2,48,1152]{2,1,0:T(8,128)(2,1)S(1)}, bf16[2,48,1152]{2,1,0:T(8,128)(2,1)S(1)}, u32[]{:S(2)}, u32[]{:S(2)}) collective-permute-start(bf16[2,48,1152]{2,1,0:T(8,128)(2,1)S(1)} %slice.540), channel_id=1, source_target_pairs={{0,16},{4,20},{8,24},{12,28},{16,0},{20,4},{24,8},{28,12},{1,17},{... | collective-permute-start | bytes 663560 | tf_op jit(solution)/shard_map/ppermute | solution.py:105
  750.1 20.1 %all-to-all-start.2 = ((f32[32,1,312]{2,1,0:T(1,128)}), f32[32,1,312]{2,1,0:T(1,128)S(1)}, u32[]{:S(2)}, u32[]{:S(2)}) async-start(f32[32,1,312]{2,1,0:T(1,128)} %all_to_all.22), calls=%async_computation.2 | async-start | bytes 98304 | tf_op jit(solution)/shard_map/all_to_all | solution.py:135
  758.4 23.7 %collective-permute-start.31 = (bf16[896,768]{1,0:T(8,128)(2,1)}, bf16[896,768]{1,0:T(8,128)(2,1)}, u32[]{:S(2)}, u32[]{:S(2)}) collective-permute-start(bf16[896,768]{1,0:T(8,128)(2,1)} %add_convert_fusion), channel_id=1, source_target_pairs={{0,0},{1,2},{2,1},{3,3},{4,4},{5,6},{6,5},{7,7},{8,8},{9,10},{10,9... | collective-permute-start | bytes 4128776 | tf_op jit(solution)/shard_map/ppermute | solution.py:88
  772.4 8.6 %collective-permute-start.36 = (bf16[48,1152]{1,0:T(8,128)(2,1)S(1)}, bf16[48,1152]{1,0:T(8,128)(2,1)S(1)}, u32[]{:S(2)}, u32[]{:S(2)}) collective-permute-start(bf16[48,1152]{1,0:T(8,128)(2,1)S(1)} %get-tuple-element.348), channel_id=1, source_target_pairs={{1,0},{0,2},{2,3},{3,1},{5,4},{4,6},{6,7},{7,5},{9,8},{8,10},{10,1... | collective-permute-start | bytes 331784 | tf_op jit(solution)/shard_map/ppermute | solution.py:123
  (112 other events, 1308.2 us)
